TPU v7x, 32 devices: a whole 2x2x4 slice. The times are simulated.
32 devices in a mesh: gz: 8 (over z, x), gy: 2 (over core), gx: 2 (over y).
Axes of the slice: x: 2, y: 2, z: 4, core: 2. Of those that a mesh axis runs over, the one named last changes fastest.
Arguments:
- positions: float32 [2048, 3, 128], P(('gz', 'gy', 'gx')), may hold values from 0 to 4
- velocities: float32 [2048, 3, 128], P(('gz', 'gy', 'gx')), may hold values from -6 to 6
- charges: float32 [2048, 128], P(('gz', 'gy', 'gx')), may hold values from -4 to 4
- atom_types: int32 [2048, 128], P(('gz', 'gy', 'gx')), may hold values from 0 to 15
- type_radius: float32 [16], replicated, may hold values from 0.3 to 1
- tiles: int32 [8192, 2], P(('gz', 'gy', 'gx')), may hold values from 0 to 383
- tile_live: int32 [32], P(('gz', 'gy', 'gx')), may hold values from 32 to 256, as said below
- destinations: int32 [2048, 1], P(('gz', 'gy', 'gx')), may hold values from 0 to 7; in each aligned block of 64 rows (0 to 63, 64 to 127, ...) at most 16 rows name the same one
Outputs:
- forces: float32 [2048, 3, 128], P(('gz', 'gy', 'gx'))
- arrived: float32 [4096, 8, 128], P(('gz', 'gy', 'gx'))
Inputs may be any that keep to these rules, and one draw needn't show every extreme that they name: Each device's used tiles are the first tile_live entries of its list; some device uses all 256. `destinations`: among the rows of one device, at most 16 name the same destination; some destination gets exactly 16 from some device.
All inputs are finite; a program needn't handle non-finite values.
Results may differ from a plain program's by a relative error of at most 0.0003.
Values sent between devices are 32-bit elements; how exact they have to be, the bound alone decides.
No kernel may reach another device: no remote copies, remote signals or barrier semaphores. Data moves between devices by JAX's collectives and lax.ppermute only.
A program may use at most 64 MiB of HBM per device.

v0:
```python
import jax
import jax.numpy as jnp
from jax import lax
from jax.sharding import PartitionSpec as P

STEPS = 2


coulomb = 0.3
time_step = 0.05
tile_group = 8


def from_partner(array, axis, bit):
    return lax.ppermute(array, axis, [(i, i ^ 1 << bit) for i in range(lax.axis_size(axis))])


def extended(cells, sides, width):
    for axis, dim in sides:
        count = lax.axis_size(axis)
        head = lax.slice_in_dim(cells, 0, width, axis=dim)
        tail = lax.slice_in_dim(cells, cells.shape[dim] - width, cells.shape[dim], axis=dim)
        cells = jnp.concatenate(
            [
                lax.ppermute(tail, axis, [(i, (i + 1) % count) for i in range(count)]),
                cells,
                lax.ppermute(head, axis, [((i + 1) % count, i) for i in range(count)]),
            ],
            axis=dim,
        )
    return cells


def passed_along(value, axis, steps):
    count = lax.axis_size(axis)
    pairs = [(source, (source + steps) % count) for source in range(count)]
    return lax.ppermute(value, axis, pairs)


def tile_forces(packed, tile_pairs, live_count):
    group_count = tile_pairs.shape[0] // tile_group

    def one_group(group_index, totals):
        first_tile = group_index * tile_group
        chosen = lax.dynamic_slice_in_dim(tile_pairs, first_tile, tile_group, 0)
        left_ids = chosen[:, 0]
        right_ids = chosen[:, 1]
        active = (first_tile + jnp.arange(tile_group, dtype=jnp.int32) < live_count).astype(
            jnp.float32
        )
        left_atoms = packed[left_ids]
        right_atoms = packed[right_ids]
        offset = left_atoms[:, 0:3, :, None] - right_atoms[:, 0:3, None, :]
        dist_sq = jnp.sum(offset * offset, axis=1)
        soften = left_atoms[:, 4, :, None] + right_atoms[:, 4, None, :]
        denominator = dist_sq + soften * soften
        strength = (
            coulomb
            * left_atoms[:, 3, :, None]
            * right_atoms[:, 3, None, :]
            / (denominator * jnp.sqrt(denominator))
        )
        strength = strength * active[:, None, None]
        pushed = strength[:, None] * offset
        on_left = jnp.sum(pushed, axis=3)
        on_right = -jnp.sum(pushed, axis=2)
        return totals.at[left_ids].add(on_left).at[right_ids].add(on_right)

    zeros = jnp.zeros((packed.shape[0], 3, packed.shape[2]), jnp.float32)
    return lax.fori_loop(0, group_count, one_group, zeros)


def local(positions, velocities, charges, atom_types, type_radius, tiles, tile_live, destinations):
    clusters = positions.shape[0]
    width = positions.shape[2]
    type_ids = jnp.arange(type_radius.shape[0], dtype=jnp.int32)
    atom_radii = jnp.sum(jnp.where(atom_types[..., None] == type_ids, type_radius, 0.0), axis=-1)
    live_count = tile_live[0]
    places = positions
    moving = velocities
    forces = jnp.zeros_like(positions)
    for step_index in range(STEPS):
        packed = jnp.concatenate([places, charges[:, None], atom_radii[:, None]], axis=1)
        row_y = lax.axis_index("gy")
        col_x = lax.axis_index("gx")
        partner = from_partner(packed, "gy", 0)
        first_row = jnp.where(row_y == 0, packed, partner)
        second_row = jnp.where(row_y == 0, partner, packed)
        column = jnp.stack([first_row, second_row])
        across = from_partner(column, "gx", 0)
        left_column = jnp.where(col_x == 0, column, across)
        right_column = jnp.where(col_x == 0, across, column)
        plate_rows = jnp.stack([left_column, right_column], axis=1).reshape(4 * clusters, 5, width)
        tower_rows = extended(packed, (("gz", 0),), clusters)
        buffer = jnp.concatenate(
            [plate_rows, tower_rows[:clusters], tower_rows[2 * clusters :]], axis=0
        )
        partial_value = tile_forces(buffer, tiles, live_count)
        plate_size = plate_rows.shape[0]
        home_forces = lax.psum_scatter(
            partial_value[:plate_size], ("gy", "gx"), scatter_dimension=0, tiled=True
        )
        returning = (
            (-1, partial_value[plate_size : plate_size + clusters]),
            (1, partial_value[plate_size + clusters :]),
        )
        for towards, portion in returning:
            home_forces = home_forces + passed_along(portion, "gz", towards)
        forces = home_forces
        moving = moving + time_step * forces
        places = places + time_step * moving
    carried = jnp.concatenate([places, moving, charges[:, None], atom_radii[:, None]], axis=1)
    groups = lax.axis_size("gz")
    capacity = max(2, 2 * clusters // groups)
    slot_count = groups * capacity
    target_ids = destinations[:, 0]
    onehot = (target_ids[:, None] == jnp.arange(groups, dtype=jnp.int32)[None, :]).astype(jnp.int32)
    rank_before = jnp.cumsum(onehot, axis=0) - onehot
    position = jnp.sum(rank_before * onehot, axis=1) + target_ids * capacity
    select = (position[None, :] == jnp.arange(slot_count, dtype=jnp.int32)[:, None]).astype(
        jnp.float32
    )
    sent_slots = jnp.einsum("sc,cfa->sfa", select, carried, precision=lax.Precision.HIGHEST)
    received = lax.all_to_all(
        sent_slots.reshape(groups, capacity, 8, width),
        "gz",
        split_axis=0,
        concat_axis=0,
        tiled=True,
    )
    return (forces, received.reshape(slot_count, 8, width))


def solution(mesh):
    placed = (
        P(("gz", "gy", "gx"), None, None),
        P(("gz", "gy", "gx"), None, None),
        P(("gz", "gy", "gx"), None),
        P(("gz", "gy", "gx"), None),
        P(),
        P(("gz", "gy", "gx"), None),
        P(("gz", "gy", "gx")),
        P(("gz", "gy", "gx"), None),
    )
    return jax.shard_map(
        local,
        mesh=mesh,
        in_specs=placed,
        out_specs=(P(("gz", "gy", "gx"), None, None), P(("gz", "gy", "gx"), None, None)),
        check_vma=False,
    )
```

profile of v0, /device:TPU:0, one launch (start us, length us, event | category | flops | bytes accessed | tf_op | source)
XLA Modules:
  0.0 458.4 jit_solution(12762817763298768254)
XLA Ops:
  9.7 1.0 collective-permute-done
  11.7 2.9 collective-permute-start.1
  14.6 1.5 collective-permute-start.2
  16.1 3.2 collective-permute-start.3
  19.4 3.3 collective-permute-done.1
  23.5 1.8 collective-permute-done.3
  26.2 172.8 %while.26 = (s32[]{:T(128)}, f32[384,3,128]{2,1,0:T(4,128)S(1)}, s32[256,2]{0,1:T(2,128)S(1)}, f32[384,5,128]{2,1,0:T(8,128)S(1)}, s32[]{:T(128)}, /*index=5*/s32[]{:T(128)}, s32[]{:T(128)}, s32[]{:T(128)}, s32[]{:T(128)}) while((s32[]{:T(128)}, f32[384,3,128]{2,1,0:T(4,128)S(1)}, s32[256,2]{0,1:T(2,128)S(1)}, f32[384,5,128]{2,1,0:T(8,128)S(1)}, ...), condition=%wide.region_7.8_spmd, body=%wide.region_1.7_spmd.sunk | while | flops 3545166 | bytes 2458263 | solution.py:70
  66.8 1.0 fusion.45
  83.0 1.0 fusion.45
  120.8 1.0 fusion.45
  142.4 1.0 fusion.45
  158.6 1.0 fusion.45
  174.8 1.0 fusion.45
  200.0 3.4 collective-permute-start.4
  203.3 2.2 collective-permute-done.4
  205.5 5.1 %collective-permute-done.5 = f32[64,3,128]{2,0,1:T(8,128)S(1)} collective-permute-done((f32[64,3,128]{2,0,1:T(8,128)S(1)}, f32[64,3,128]{2,0,1:T(8,128)S(1)}, u32[]{:S(2)}, u32[]{:S(2)}) %collective-permute-start.5) | collective-permute-done | bytes 98336 | tf_op jit(solution)/shard_map/ppermute | solution.py:37
  210.6 9.3 %reduce-scatter.3.cloned.1.call-done = f32[64,3,128]{2,0,1:T(8,128)} async-done(((f32[256,3,128]{2,0,1:T(8,128)}), f32[64,3,128]{2,0,1:T(8,128)}) %reduce-scatter.3.cloned.1.call-update) | async-done | bytes 98320 | tf_op jit(solution)/shard_map/reduce_scatter | solution.py:100
  221.0 1.4 collective-permute-done.6
  222.8 1.7 collective-permute-start.8
  224.5 3.0 collective-permute-start.9
  227.5 4.7 %collective-permute-done.7 = f32[2,64,5,128]{3,1,2,0:T(8,128)S(1)} collective-permute-done((f32[2,64,5,128]{3,1,2,0:T(8,128)S(1)}, f32[2,64,5,128]{3,1,2,0:T(8,128)S(1)}, u32[]{:S(2)}, u32[]{:S(2)}) %collective-permute-start.7) | collective-permute-done | bytes 327712 | tf_op jit(solution)/shard_map/ppermute | solution.py:15
  232.4 1.3 collective-permute-done.9
  234.5 172.7 %while.27 = (s32[]{:T(128)}, f32[384,3,128]{2,1,0:T(4,128)S(1)}, s32[256,2]{0,1:T(2,128)S(1)}, f32[384,5,128]{2,1,0:T(8,128)S(1)}, s32[]{:T(128)}, /*index=5*/s32[]{:T(128)}, s32[]{:T(128)}, s32[]{:T(128)}, s32[]{:T(128)}) while((s32[]{:T(128)}, f32[384,3,128]{2,1,0:T(4,128)S(1)}, s32[256,2]{0,1:T(2,128)S(1)}, ...), condition=%wide.region_15.16_spmd, body=%wide.region_9.15_spmd.sunk | while | flops 3545166 | bytes 2458263 | solution.py:70
  248.1 1.0 fusion.50
  269.7 1.0 fusion.50
  291.3 1.0 fusion.50
  408.5 3.1 collective-permute-start.10
  411.6 2.2 collective-permute-done.10
  413.8 5.1 %collective-permute-done.11 = f32[64,3,128]{2,0,1:T(8,128)S(1)} collective-permute-done((f32[64,3,128]{2,0,1:T(8,128)S(1)}, f32[64,3,128]{2,0,1:T(8,128)S(1)}, u32[]{:S(2)}, u32[]{:S(2)}) %collective-permute-start.11) | collective-permute-done | bytes 98336 | tf_op jit(solution)/shard_map/ppermute | solution.py:37
  418.9 9.9 %reduce-scatter.5.cloned.1.call-done = f32[64,3,128]{2,0,1:T(8,128)} async-done(((f32[256,3,128]{2,0,1:T(8,128)}), f32[64,3,128]{2,0,1:T(8,128)}) %reduce-scatter.5.cloned.1.call-update) | async-done | bytes 98320 | tf_op jit(solution)/shard_map/reduce_scatter | solution.py:100
  428.8 1.6 multiply_add_fusion
  430.9 19.7 %all_to_all.5 = f32[8,16,8,128]{3,1,2,0:T(8,128)S(1)} all-to-all(f32[8,16,8,128]{3,1,2,0:T(8,128)S(1)} %copy.65), channel_id=1, replica_groups=mesh['gz'=8,'gy'=2,'gx'=2] {'gz'}, dimensions={0} | all-to-all | bytes 1048576 | tf_op jit(solution)/shard_map/all_to_all | solution.py:124
  (1069 shorter events, 340.3 us)
Async XLA Ops:
  7.2 212.8 %reduce-scatter.3.cloned.1.call-start = ((), (), s32[]{:S(2)}) async-start(), calls=%async_computation.3 | async-start | bytes 491520 | tf_op jit(solution)/shard_map/reduce_scatter | solution.py:100
  9.1 1.6 collective-permute-start
  11.7 11.0 %collective-permute-start.1 = (f32[2,64,5,128]{3,1,2,0:T(8,128)S(1)}, f32[2,64,5,128]{3,1,2,0:T(8,128)S(1)}, u32[]{:S(2)}, u32[]{:S(2)}) collective-permute-start(f32[2,64,5,128]{3,1,2,0:T(8,128)S(1)} %pad_maximum_fusion.4), channel_id=1, source_target_pairs={{0,1},{1,0},{2,3},{3,2},{4,5},{5,4},{6,7},{7,6},{8,9},{9,8},{10,11... | collective-permute-start | bytes 983048 | tf_op jit(solution)/shard_map/ppermute | solution.py:15
  14.6 8.9 %collective-permute-start.2 = (f32[64,5,128]{2,0,1:T(8,128)S(1)}, f32[64,5,128]{2,0,1:T(8,128)S(1)}, u32[]{:S(2)}, u32[]{:S(2)}) collective-permute-start(f32[64,5,128]{2,0,1:T(8,128)S(1)} %pad_maximum_fusion.7), channel_id=1, source_target_pairs={{0,4},{4,8},{8,12},{12,16},{16,20},{20,24},{24,28},{28,0},{1,5},{5... | collective-permute-start | bytes 491528 | tf_op jit(solution)/shard_map/ppermute | solution.py:25
  16.1 9.2 %collective-permute-start.3 = (f32[64,5,128]{2,0,1:T(8,128)S(1)}, f32[64,5,128]{2,0,1:T(8,128)S(1)}, u32[]{:S(2)}, u32[]{:S(2)}) collective-permute-start(f32[64,5,128]{2,0,1:T(8,128)S(1)} %pad_maximum_fusion.7), channel_id=1, source_target_pairs={{4,0},{8,4},{12,8},{16,12},{20,16},{24,20},{28,24},{0,28},{5,1},{9... | collective-permute-start | bytes 491528 | tf_op jit(solution)/shard_map/ppermute | solution.py:27
  25.4 0.7 copy-start.3
  199.0 20.9 %copy-start = (f32[64,3,128]{2,0,1:T(8,128)S(1)}, f32[64,3,128]{2,0,1:T(8,128)}, u32[]{:S(2)}) copy-start(f32[64,3,128]{2,0,1:T(8,128)} %param.12) | copy-start | bytes 294916
  199.0 20.9 %copy-start.2 = (f32[64,3,128]{2,0,1:T(8,128)S(1)}, f32[64,3,128]{2,0,1:T(8,128)}, u32[]{:S(2)}) copy-start(f32[64,3,128]{2,0,1:T(8,128)} %param.13) | copy-start | bytes 294916
  199.0 21.8 %copy-start.1 = (f32[64,128]{1,0:T(8,128)S(1)}, f32[64,128]{1,0:T(8,128)}, u32[]{:S(2)}) copy-start(f32[64,128]{1,0:T(8,128)} %param.14) | copy-start | bytes 98308
  199.9 228.9 %reduce-scatter.5.cloned.1.call-start = ((), (), s32[]{:S(2)}) async-start(), calls=%async_computation.4 | async-start | bytes 491520 | tf_op jit(solution)/shard_map/reduce_scatter | solution.py:100
  200.0 5.6 %collective-permute-start.4 = (f32[64,3,128]{2,0,1:T(8,128)S(1)}, f32[64,3,128]{2,0,1:T(8,128)S(1)}, u32[]{:S(2)}, u32[]{:S(2)}) collective-permute-start(f32[64,3,128]{2,0,1:T(8,128)S(1)} %get-tuple-element.283), channel_id=1, source_target_pairs={{0,28},{4,0},{8,4},{12,8},{16,12},{20,16},{24,20},{28,24},{1,29},{... | collective-permute-start | bytes 294920 | tf_op jit(solution)/shard_map/ppermute | solution.py:37
  203.3 7.3 %collective-permute-start.5 = (f32[64,3,128]{2,0,1:T(8,128)S(1)}, f32[64,3,128]{2,0,1:T(8,128)S(1)}, u32[]{:S(2)}, u32[]{:S(2)}) collective-permute-start(f32[64,3,128]{2,0,1:T(8,128)S(1)} %get-tuple-element.284), channel_id=1, source_target_pairs={{0,4},{4,8},{8,12},{12,16},{16,20},{20,24},{24,28},{28,0},{1,5},{5... | collective-permute-start | bytes 294920 | tf_op jit(solution)/shard_map/ppermute | solution.py:37
  220.9 1.5 collective-permute-start.6
  222.4 9.8 %collective-permute-start.7 = (f32[2,64,5,128]{3,1,2,0:T(8,128)S(1)}, f32[2,64,5,128]{3,1,2,0:T(8,128)S(1)}, u32[]{:S(2)}, u32[]{:S(2)}) collective-permute-start(f32[2,64,5,128]{3,1,2,0:T(8,128)S(1)} %pad_maximum_fusion.5), channel_id=1, source_target_pairs={{0,1},{1,0},{2,3},{3,2},{4,5},{5,4},{6,7},{7,6},{8,9},{9,8},{10,11... | collective-permute-start | bytes 983048 | tf_op jit(solution)/shard_map/ppermute | solution.py:15
  222.8 9.6 %collective-permute-start.8 = (f32[64,5,128]{2,0,1:T(8,128)S(1)}, f32[64,5,128]{2,0,1:T(8,128)S(1)}, u32[]{:S(2)}, u32[]{:S(2)}) collective-permute-start(f32[64,5,128]{2,0,1:T(8,128)S(1)} %pad_maximum_fusion.6), channel_id=1, source_target_pairs={{0,4},{4,8},{8,12},{12,16},{16,20},{20,24},{24,28},{28,0},{1,5},{5... | collective-permute-start | bytes 491528 | tf_op jit(solution)/shard_map/ppermute | solution.py:25
  224.5 9.2 %collective-permute-start.9 = (f32[64,5,128]{2,0,1:T(8,128)S(1)}, f32[64,5,128]{2,0,1:T(8,128)S(1)}, u32[]{:S(2)}, u32[]{:S(2)}) collective-permute-start(f32[64,5,128]{2,0,1:T(8,128)S(1)} %pad_maximum_fusion.6), channel_id=1, source_target_pairs={{4,0},{8,4},{12,8},{16,12},{20,16},{24,20},{28,24},{0,28},{5,1},{9... | collective-permute-start | bytes 491528 | tf_op jit(solution)/shard_map/ppermute | solution.py:27
  407.3 0.9 copy-start.4
  408.5 5.3 %collective-permute-start.10 = (f32[64,3,128]{2,0,1:T(8,128)S(1)}, f32[64,3,128]{2,0,1:T(8,128)S(1)}, u32[]{:S(2)}, u32[]{:S(2)}) collective-permute-start(f32[64,3,128]{2,0,1:T(8,128)S(1)} %get-tuple-element.281), channel_id=1, source_target_pairs={{0,28},{4,0},{8,4},{12,8},{16,12},{20,16},{24,20},{28,24},{1,29},{... | collective-permute-start | bytes 294920 | tf_op jit(solution)/shard_map/ppermute | solution.py:37
  411.6 7.3 %collective-permute-start.11 = (f32[64,3,128]{2,0,1:T(8,128)S(1)}, f32[64,3,128]{2,0,1:T(8,128)S(1)}, u32[]{:S(2)}, u32[]{:S(2)}) collective-permute-start(f32[64,3,128]{2,0,1:T(8,128)S(1)} %get-tuple-element.282), channel_id=1, source_target_pairs={{0,4},{4,8},{8,12},{12,16},{16,20},{20,24},{24,28},{28,0},{1,5},{5... | collective-permute-start | bytes 294920 | tf_op jit(solution)/shard_map/ppermute | solution.py:37
Sparse Core Ops, SparseCore 0:
  200.0 19.8 reduce-scatter.2
  408.2 20.5 reduce-scatter.4
where the time goes:
time: 459 us; the launch traced here: 458 us
  other arithmetic  267 us (58%)
  local copies, waits for them, and re-layouts  81.2 us (18%)
  waiting for transfers between devices  48 us (10%)
  starting transfers between devices  20 us (4%)
  blocking collectives  19.7 us (4%)
  between operations  14.3 us (3%)
  loops' own time  7.34 us (2%)
    scatter-add x128, other arithmetic, one_group(): return totals.at[left_ids].add(on_left).at[right_ids].add(on_right)  99.8 us
    reduce_sum x64, other arithmetic, one_group(): on_right = -jnp.sum(pushed, axis=2)  64.2 us
    convert_element_type x64, other arithmetic, one_group(): (first_tile + jnp.arange(tile_group, dtype=jnp.int32) < live_count).astyp...  41.7 us
    gather x64, local copies, waits for them, and re-layouts, one_group(): left_atoms = packed[left_ids]  35.5 us
    gather x64, local copies, waits for them, and re-layouts, one_group(): right_atoms = packed[right_ids]  35.4 us
    reduce_sum x64, other arithmetic, one_group(): dist_sq = jnp.sum(offset * offset, axis=1)  30.2 us
    mul x64, other arithmetic, one_group(): strength = strength * active[:, None, None]  23.1 us
    all_to_all x1, blocking collectives, local(): lax.all_to_all(sent_slots.reshape(groups, capacity, 8, width), 'gz', spli...  19.7 us
  transfers between devices with their start and end apart: 14, of which 13 were waited for; matrix products, arithmetic and copies ran while one was open for 0% of the time, Pallas kernels for 0%

commit v1 on v0

v1 whole, which is shorter than its diff:
```python
import functools

import jax
import jax.numpy as jnp
from jax import lax
from jax.experimental import pallas as pl
from jax.experimental.pallas import tpu as pltpu
from jax.sharding import PartitionSpec as P

STEPS = 2

coulomb = 0.3
time_step = 0.05
middle = 2.0
feature_rows = 33
moment_rows = 9
unroll = 16


def shifted(value, axis, steps):
    count = lax.axis_size(axis)
    return lax.ppermute(value, axis, [(i, (i + steps) % count) for i in range(count)])


def rounded(value):
    return value.astype(jnp.bfloat16).astype(jnp.float32)


def tile_kernel(clusters, *refs):
    pairs, live = refs[0:2]
    places = refs[2:8]
    fixed = refs[8:14]
    forces = refs[14:20]
    features, moments, totals, squares, highs, lows, turned_highs, turned_lows = refs[20:28]
    width = features.shape[1]
    ones = jnp.ones((clusters, width), jnp.float32)
    none = jnp.zeros((clusters, width), jnp.float32)
    for piece in range(6):
        first = piece * clusters

        def put(row, value):
            features[pl.ds(first * feature_rows + row, clusters, stride=feature_rows), :] = value

        charge = fixed[piece][3]
        square = none
        for part in range(4):
            value = places[piece][part] - middle if part < 3 else fixed[piece][4]
            square = square + value * value
            high = rounded(value)
            rest = value - high
            mid = rounded(rest)
            low = rounded(rest - mid)
            put(part, high)
            put(4 + part, mid)
            put(8 + part, high)
            put(12 + part, low)
            put(16 + part, high)
            weighed = charge * value if part < 3 else charge
            weighed_high = rounded(weighed)
            base = first * moment_rows + part
            moments[pl.ds(base, clusters, stride=moment_rows), :] = weighed_high
            moments[pl.ds(base + 4, clusters, stride=moment_rows), :] = rounded(weighed - weighed_high)
        high = rounded(square)
        rest = square - high
        mid = rounded(rest)
        for row, value in enumerate((high, mid, rounded(rest - mid), none)):
            put(20 + row, value)
            put(24 + row, ones if row < 3 else none)
            put(28 + row, value)
    totals[...] = jnp.zeros_like(totals)
    squares[...] = jnp.ones_like(squares)
    highs[...] = jnp.zeros_like(highs)
    lows[...] = jnp.zeros_like(lows)
    turned_highs[...] = jnp.zeros_like(highs)
    turned_lows[...] = jnp.zeros_like(lows)
    row = lax.broadcasted_iota(jnp.int32, (24, width), 0) % 4
    scale = jnp.where(row == 3, 2.0, -2.0)
    last = pairs.shape[0] // 2 - 1

    def ends(t):
        t = jnp.clip(t, 0, last)
        return pairs[2 * t], pairs[2 * t + 1]

    def features_of(t):
        left, right = ends(t)
        left_base = left * feature_rows
        right_base = right * feature_rows
        pair_a = features[pl.ds(left_base, 8), :]
        streamed = jnp.concatenate([pair_a, pair_a, features[pl.ds(left_base + 8, 8), :]], axis=0) * scale
        streamed = jnp.concatenate([streamed, features[pl.ds(left_base + 20, 8), :]], axis=0)
        kept = jnp.concatenate(
            [
                features[pl.ds(right_base, 8), :],
                features[pl.ds(right_base + 4, 8), :],
                features[pl.ds(right_base + 12, 8), :],
                features[pl.ds(right_base + 24, 8), :],
            ],
            axis=0,
        )
        return streamed.astype(jnp.bfloat16), kept.astype(jnp.bfloat16)

    def prepared(t):
        streamed, kept = zip(features_of(t), features_of(t + 1))
        apart = jnp.zeros_like(kept[0])
        kept = jnp.concatenate(
            [jnp.concatenate([kept[0], apart], axis=1), jnp.concatenate([apart, kept[1]], axis=1)], axis=0
        )
        return jnp.concatenate(streamed, axis=0).T, kept

    def distances(streamed, kept, slot):
        square = lax.dot_general(
            streamed,
            kept,
            (((1,), (0,)), ((), ())),
            preferred_element_type=jnp.float32,
        )
        squares[slot] = square[:, :width]
        squares[slot + 1] = square[:, width:]

    def strengths(slot):
        inverse = lax.rsqrt(squares[slot])
        strength = inverse * inverse * inverse
        high = strength.astype(jnp.bfloat16)
        low = (strength - high.astype(jnp.float32)).astype(jnp.bfloat16)
        highs[slot] = high
        lows[slot] = low
        turned_highs[slot] = high.T
        turned_lows[slot] = low.T

    def pushes(t, slot):
        left, right = ends(t)
        left_at = left * moment_rows
        right_at = right * moment_rows
        weight = jnp.where((t >= 0) & (t < live[0]), 1.0, 0.0)
        both = jnp.concatenate([moments[pl.ds(left_at, 8), :], moments[pl.ds(right_at, 8), :]], axis=0)
        both = (both * weight).astype(jnp.bfloat16)
        turned = jnp.concatenate([turned_highs[slot], turned_lows[slot]], axis=1)
        straight = jnp.concatenate([highs[slot], lows[slot]], axis=1)
        on_left = jnp.dot(both, turned, preferred_element_type=jnp.float32)
        on_right = jnp.dot(both, straight, preferred_element_type=jnp.float32)
        on_left = on_left[8:]
        on_right = on_right[:8]
        return left_at, right_at, on_left[:, :width] + on_left[:, width:], on_right[:, :width] + on_right[:, width:]

    def group(g, carry):
        first = g * unroll
        ready = [prepared(first + u) for u in range(0, unroll, 2)]
        pushed = [pushes(first + u - 2 * unroll, u) for u in range(unroll)]
        for u in range(unroll):
            strengths(u)
        for u in range(0, unroll, 2):
            distances(*ready[u // 2], u)
        for left_at, right_at, on_left, on_right in pushed:
            totals[pl.ds(left_at, 8), :] += on_left
            totals[pl.ds(right_at, 8), :] += on_right
        return carry

    lax.fori_loop(0, (live[0] + unroll - 1) // unroll + 2, group, 0)
    for piece in range(6):
        first = piece * clusters * moment_rows

        def total(row):
            return (
                totals[pl.ds(first + row, clusters, stride=moment_rows), :]
                + totals[pl.ds(first + row + 4, clusters, stride=moment_rows), :]
            )

        charge = coulomb * fixed[piece][3]
        summed = total(3)
        for part in range(3):
            forces[piece][part] = charge * ((places[piece][part] - middle) * summed - total(part))


def tile_forces(pairs, live, places, fixed):
    _, clusters, width = places[0].shape
    smem = pl.BlockSpec(memory_space=pltpu.SMEM)
    vmem = pl.BlockSpec(memory_space=pltpu.VMEM)
    return pl.pallas_call(
        functools.partial(tile_kernel, clusters),
        out_shape=[jax.ShapeDtypeStruct((3, clusters, width), jnp.float32)] * 6,
        in_specs=[smem, smem] + [vmem] * 12,
        out_specs=[vmem] * 6,
        scratch_shapes=[
            pltpu.VMEM((6 * clusters * feature_rows, width), jnp.float32),
            pltpu.VMEM((6 * clusters * moment_rows, width), jnp.float32),
            pltpu.VMEM((6 * clusters * moment_rows, width), jnp.float32),
            pltpu.VMEM((unroll, width, width), jnp.float32),
            pltpu.VMEM((unroll, width, width), jnp.bfloat16),
            pltpu.VMEM((unroll, width, width), jnp.bfloat16),
            pltpu.VMEM((unroll, width, width), jnp.bfloat16),
            pltpu.VMEM((unroll, width, width), jnp.bfloat16),
        ],
        compiler_params=pltpu.CompilerParams(vmem_limit_bytes=40 << 20),
        name="tile_forces",
    )(pairs, live, *places, *fixed)


def imported(value):
    over_x = shifted(value, "gx", 1)
    return [
        value,
        over_x,
        shifted(value, "gy", 1),
        shifted(over_x, "gy", 1),
        shifted(value, "gz", 1),
        shifted(value, "gz", -1),
    ]


def returned(partial):
    below = shifted(partial[4], "gz", -1)
    above = shifted(partial[5], "gz", 1)
    direct = shifted(partial[2], "gy", 1)
    beyond = shifted(partial[3], "gy", 1)
    across = shifted(partial[1] + beyond, "gx", 1)
    return partial[0] + direct + across + below + above


def local(positions, velocities, charges, atom_types, type_radius, tiles, tile_live, destinations):
    clusters = positions.shape[0]
    width = positions.shape[2]
    type_ids = jnp.arange(type_radius.shape[0], dtype=jnp.int32)
    atom_radii = jnp.sum(jnp.where(atom_types[..., None] == type_ids, type_radius, 0.0), axis=-1)
    mine = lax.axis_index("gy") * lax.axis_size("gx") + lax.axis_index("gx")
    block = tiles // clusters
    block = jnp.where(block < 4, block ^ mine, block)
    pairs = (block * clusters + tiles % clusters).reshape(-1)
    places = jnp.transpose(positions, (1, 0, 2))
    moving = jnp.transpose(velocities, (1, 0, 2))
    home = jnp.concatenate([places, charges[None], atom_radii[None]], axis=0)
    fixed = imported(home)
    current = fixed
    for step_index in range(STEPS):
        if step_index:
            current = imported(places)
        forces = returned(tile_forces(pairs, tile_live, current, fixed))
        moving = moving + time_step * forces
        places = places + time_step * moving
    carried = jnp.concatenate([places, moving, charges[None], atom_radii[None]], axis=0)
    groups = lax.axis_size("gz")
    capacity = max(2, 2 * clusters // groups)
    slot_count = groups * capacity
    target_ids = destinations[:, 0]
    onehot = (target_ids[:, None] == jnp.arange(groups, dtype=jnp.int32)[None, :]).astype(jnp.int32)
    rank_before = jnp.cumsum(onehot, axis=0) - onehot
    position = jnp.sum(rank_before * onehot, axis=1) + target_ids * capacity
    select = (position[None, :] == jnp.arange(slot_count, dtype=jnp.int32)[:, None]).astype(jnp.float32)
    sent_slots = jnp.einsum("sc,fca->sfa", select, carried, precision=lax.Precision.HIGHEST)
    received = lax.all_to_all(
        sent_slots.reshape(groups, capacity, 8, width), "gz", split_axis=0, concat_axis=0, tiled=True
    )
    return (jnp.transpose(forces, (1, 0, 2)), received.reshape(slot_count, 8, width))


def solution(mesh):
    whole = ("gz", "gy", "gx")
    placed = (
        P(whole, None, None),
        P(whole, None, None),
        P(whole, None),
        P(whole, None),
        P(),
        P(whole, None),
        P(whole),
        P(whole, None),
    )
    return jax.shard_map(
        local,
        mesh=mesh,
        in_specs=placed,
        out_specs=(P(whole, None, None), P(whole, None, None)),
        check_vma=False,
    )
```

time: 459 us -> 90.7 us (0.20)
  other arithmetic: 267 us -> 3.03 us
  local copies, waits for them, and re-layouts: 81.2 us -> 1.93 us
  waiting for transfers between devices: 48 us -> 18.3 us
  Pallas kernels: 0 us -> 24.9 us
  between operations: 14.3 us -> 1.46 us
  loops' own time: 7.34 us -> 0 us
    scatter-add x128 -> x0, other arithmetic: 99.8 us -> none  [one_group(): return totals.at[left_ids].add(on_left).at[right_ids].add(on_right)]
    reduce_sum x128 -> x0, other arithmetic: 94.5 us -> none  [the longest x64 64.2 us: one_group(): on_right = -jnp.sum(pushed, axis=2)]
    gather x128 -> x0, local copies, waits for them, and re-layouts: 70.9 us -> none  [the longest x64 35.5 us: one_group(): left_atoms = packed[left_ids]]
    convert_element_type x64 -> x0, other arithmetic: 41.7 us -> none  [one_group(): (first_tile + jnp.arange(tile_group, dtype=jnp.int32) < live_count).astyp...]
    pallas_call x0 -> x2, Pallas kernels: none -> 24.9 us  [tile_forces(): pl.pallas_call(functools.partial(tile_kernel, clusters), out_shape=[jax.S...]
    mul x128 -> x0, other arithmetic: 23.9 us -> none  [the longest x64 23.1 us: one_group(): strength = strength * active[:, None, None]]
    reduce_scatter x2 -> x0, waiting for transfers between devices: 19.2 us -> none  [local(): lax.psum_scatter(partial_value[:plate_size], ('gy', 'gx'), scatter_dimens...]
    ppermute x12 -> x20, waiting for transfers between devices: 28.8 us -> 18.3 us  [shifted(): lax.ppermute(value, axis, [(i, (i + steps) % count) for i in range(count)])]
  transfers between devices with their start and end apart: 14 -> 20, of which waited for: 13 -> 7; matrix products, arithmetic and copies ran while one was open for 0% -> 1% of each run, Pallas kernels for 0% -> 0%
where the time goes in v1:
time: 90.7 us; the launch traced here: 90.3 us
  Pallas kernels  24.9 us (27%)
  starting transfers between devices  22.7 us (25%)
  waiting for transfers between devices  18.3 us (20%)
  blocking collectives  17.4 us (19%)
  other arithmetic  3.03 us (3%)
  local copies, waits for them, and re-layouts  1.93 us (2%)
  between operations  1.46 us (2%)
    pallas_call x2, Pallas kernels, tile_forces(): pl.pallas_call(functools.partial(tile_kernel, clusters), out_shape=[jax.S...  24.9 us
    ppermute x20, starting transfers between devices, shifted(): lax.ppermute(value, axis, [(i, (i + steps) % count) for i in range(count)])  22.7 us
    ppermute x20, waiting for transfers between devices, shifted(): lax.ppermute(value, axis, [(i, (i + steps) % count) for i in range(count)])  18.3 us
    all_to_all x1, blocking collectives, local(): lax.all_to_all(sent_slots.reshape(groups, capacity, 8, width), 'gz', spli...  17.4 us
  transfers between devices with their start and end apart: 20, of which 7 were waited for; matrix products, arithmetic and copies ran while one was open for 1% of the time, Pallas kernels for 0%

profile of v1, /device:TPU:0, one launch (start us, length us, event | category | flops | bytes accessed | tf_op | source)
XLA Modules:
  0.0 90.3 jit_solution(16305196028472738390)
XLA Ops:
  0.6 1.0 %select_reduce_fusion = f32[64,128]{1,0:T(8,128)S(1)} fusion(f32[16]{0:T(128)} %param.12, s32[64,128]{1,0:T(8,128)} %param.11), kind=kLoop, calls=%fused_computation | loop fusion | flops 385024 | bytes 65600 | tf_op jit(solution)/shard_map/reduce_sum | solution.py:223
  1.7 0.9 %pad_maximum_fusion.refs_2_.refs_8_ = f32[5,64,128]{2,1,0:T(8,128)S(1)} fusion(f32[1,64,128]{2,1,0:T(8,128)S(1)} %bitcast.18, f32[1,64,128]{2,1,0:T(8,128)S(1)} %bitcast.20, f32[3,64,128]{2,1,0:T(8,128)} %bitcast.17), kind=kLoop, calls=%fused_computation.10 | loop fusion | flops 81920 | bytes 327680 | tf_op jit(solution)/shard_map/concatenate | solution.py:230
  2.6 3.1 %collective-permute-start = (f32[5,64,128]{2,1,0:T(8,128)S(1)}, f32[5,64,128]{2,1,0:T(8,128)S(1)}, u32[]{:S(2)}, u32[]{:S(2)}) collective-permute-start(f32[5,64,128]{2,1,0:T(8,128)S(1)} %pad_maximum_fusion.refs_2_.refs_8_), channel_id=1, source_target_pairs={{0,1},{1,0},{2,3},{3,2},{4,5},{5,4},{6,7},{7,6},{8,9},{9,8},{10,11... | collective-permute-start | bytes 491528 | tf_op jit(solution)/shard_map/ppermute | solution.py:22
  5.6 1.5 %collective-permute-start.3 = (f32[5,64,128]{2,1,0:T(8,128)S(1)}, f32[5,64,128]{2,1,0:T(8,128)S(1)}, u32[]{:S(2)}, u32[]{:S(2)}) collective-permute-start(f32[5,64,128]{2,1,0:T(8,128)S(1)} %pad_maximum_fusion.refs_2_.refs_8_), channel_id=1, source_target_pairs={{0,4},{4,8},{8,12},{12,16},{16,20},{20,24},{24,28},{28,0},{1,5},{5... | collective-permute-start | bytes 491528 | tf_op jit(solution)/shard_map/ppermute | solution.py:22
  7.1 3.2 %collective-permute-start.4 = (f32[5,64,128]{2,1,0:T(8,128)S(1)}, f32[5,64,128]{2,1,0:T(8,128)S(1)}, u32[]{:S(2)}, u32[]{:S(2)}) collective-permute-start(f32[5,64,128]{2,1,0:T(8,128)S(1)} %pad_maximum_fusion.refs_2_.refs_8_), channel_id=1, source_target_pairs={{0,28},{4,0},{8,4},{12,8},{16,12},{20,16},{24,20},{28,24},{1,29},{... | collective-permute-start | bytes 491528 | tf_op jit(solution)/shard_map/ppermute | solution.py:22
  10.4 0.6 copy-done.4
  11.1 0.1 copy.18
  11.2 0.1 reshape.22.refs_0_
  12.0 3.1 %collective-permute-done.3.refs_6_.refs_12_ = f32[5,64,128]{2,1,0:T(8,128)S(1)} collective-permute-done((f32[5,64,128]{2,1,0:T(8,128)S(1)}, f32[5,64,128]{2,1,0:T(8,128)S(1)}, u32[]{:S(2)}, u32[]{:S(2)}) %collective-permute-start.3) | collective-permute-done | bytes 163872 | tf_op jit(solution)/shard_map/ppermute | solution.py:22
  15.1 1.8 %collective-permute-done.4.refs_7_.refs_13_ = f32[5,64,128]{2,1,0:T(8,128)S(1)} collective-permute-done((f32[5,64,128]{2,1,0:T(8,128)S(1)}, f32[5,64,128]{2,1,0:T(8,128)S(1)}, u32[]{:S(2)}, u32[]{:S(2)}) %collective-permute-start.4) | collective-permute-done | bytes 163872 | tf_op jit(solution)/shard_map/ppermute | solution.py:22
  17.0 12.5 %tile_forces.2 = (f32[3,64,128]{2,1,0:T(8,128)S(1)}, f32[3,64,128]{2,1,0:T(8,128)S(1)}, f32[3,64,128]{2,1,0:T(8,128)S(1)}, f32[3,64,128]{2,1,0:T(8,128)S(1)}, f3...) custom-call(s32[512]{0:T(512)S(1)} %reshape.22.refs_0_, s32[1]{0:T(128)S(6)} %copy.21.refs_1_, ...), custom_call_target="tpu_custom_call" | custom-call | tf_op jit(solution)/shard_map/tile_forces/pallas_call | solution.py:178
  29.4 0.1 collective-permute-start.6
  29.5 0.5 collective-permute-start.9
  30.1 4.2 %collective-permute-start.8 = (f32[3,64,128]{2,1,0:T(8,128)S(1)}, f32[3,64,128]{2,1,0:T(8,128)S(1)}, u32[]{:S(2)}, u32[]{:S(2)}) collective-permute-start(f32[3,64,128]{2,1,0:T(8,128)S(1)} %get-tuple-element.18), channel_id=1, source_target_pairs={{0,28},{4,0},{8,4},{12,8},{16,12},{20,16},{24,20},{28,24},{1,29},{... | collective-permute-start | bytes 294920 | tf_op jit(solution)/shard_map/ppermute | solution.py:22
  34.3 0.1 collective-permute-start.7
  34.4 3.0 %collective-permute-done.9 = f32[3,64,128]{2,1,0:T(8,128)S(1)} collective-permute-done((f32[3,64,128]{2,1,0:T(8,128)S(1)}, f32[3,64,128]{2,1,0:T(8,128)S(1)}, u32[]{:S(2)}, u32[]{:S(2)}) %collective-permute-start.9) | collective-permute-done | bytes 98336 | tf_op jit(solution)/shard_map/ppermute | solution.py:22
  37.4 2.2 %collective-permute-done.7 = f32[3,64,128]{2,1,0:T(8,128)S(1)} collective-permute-done((f32[3,64,128]{2,1,0:T(8,128)S(1)}, f32[3,64,128]{2,1,0:T(8,128)S(1)}, u32[]{:S(2)}, u32[]{:S(2)}) %collective-permute-start.7) | collective-permute-done | bytes 98336 | tf_op jit(solution)/shard_map/ppermute | solution.py:22
  39.7 0.4 collective-permute-start.10
  40.0 4.7 %collective-permute-start.14 = (f32[3,64,128]{2,1,0:T(8,128)S(1)}, f32[3,64,128]{2,1,0:T(8,128)S(1)}, u32[]{:S(2)}, u32[]{:S(2)}) collective-permute-start(f32[3,64,128]{2,1,0:T(8,128)S(1)} %get-tuple-element.29.refs_2_), channel_id=1, source_target_pairs={{0,28},{4,0},{8,4},{12,8},{16,12},{20,16},{24,20},{28,24},{1,29},{... | collective-permute-start | bytes 294920 | tf_op jit(solution)/shard_map/ppermute | solution.py:22
  44.7 0.1 fusion.8
  44.8 0.1 reduce_window_sum.11
  44.9 3.0 %collective-permute-done.13.refs_6_ = f32[3,64,128]{2,1,0:T(8,128)S(1)} collective-permute-done((f32[3,64,128]{2,1,0:T(8,128)S(1)}, f32[3,64,128]{2,1,0:T(8,128)S(1)}, u32[]{:S(2)}, u32[]{:S(2)}) %collective-permute-start.13) | collective-permute-done | bytes 98336 | tf_op jit(solution)/shard_map/ppermute | solution.py:22
  47.9 12.4 %tile_forces.3 = (f32[3,64,128]{2,1,0:T(8,128)S(1)}, f32[3,64,128]{2,1,0:T(8,128)S(1)}, f32[3,64,128]{2,1,0:T(8,128)S(1)}, f32[3,64,128]{2,1,0:T(8,128)S(1)}, f3...) custom-call(s32[512]{0:T(512)S(1)} %reshape.22.refs_0_, s32[1]{0:T(128)S(6)} %copy.21.refs_1_, ...), custom_call_target="tpu_custom_call" | custom-call | tf_op jit(solution)/shard_map/tile_forces/pallas_call | solution.py:178
  60.5 0.2 select_reduce_fusion.1
  60.6 0.3 collective-permute-start.19
  60.9 4.5 %collective-permute-start.18 = (f32[3,64,128]{2,1,0:T(8,128)S(1)}, f32[3,64,128]{2,1,0:T(8,128)S(1)}, u32[]{:S(2)}, u32[]{:S(2)}) collective-permute-start(f32[3,64,128]{2,1,0:T(8,128)S(1)} %get-tuple-element.24), channel_id=1, source_target_pairs={{0,28},{4,0},{8,4},{12,8},{16,12},{20,16},{24,20},{28,24},{1,29},{... | collective-permute-start | bytes 294920 | tf_op jit(solution)/shard_map/ppermute | solution.py:22
  65.5 3.1 %collective-permute-done.19 = f32[3,64,128]{2,1,0:T(8,128)S(1)} collective-permute-done((f32[3,64,128]{2,1,0:T(8,128)S(1)}, f32[3,64,128]{2,1,0:T(8,128)S(1)}, u32[]{:S(2)}, u32[]{:S(2)}) %collective-permute-start.19) | collective-permute-done | bytes 98336 | tf_op jit(solution)/shard_map/ppermute | solution.py:22
  68.6 2.1 %collective-permute-done.17 = f32[3,64,128]{2,1,0:T(8,128)S(1)} collective-permute-done((f32[3,64,128]{2,1,0:T(8,128)S(1)}, f32[3,64,128]{2,1,0:T(8,128)S(1)}, u32[]{:S(2)}, u32[]{:S(2)}) %collective-permute-start.17) | collective-permute-done | bytes 98336 | tf_op jit(solution)/shard_map/ppermute | solution.py:22
  70.7 0.7 multiply_add_fusion
  71.4 0.5 fusion
  71.9 17.4 %all_to_all.5 = f32[8,16,8,128]{3,1,2,0:T(8,128)S(1)} all-to-all(f32[8,16,8,128]{3,1,2,0:T(8,128)S(1)} %copy.19), channel_id=1, replica_groups=mesh['gz'=8,'gy'=2,'gx'=2] {'gz'}, dimensions={0} | all-to-all | bytes 1048576 | tf_op jit(solution)/shard_map/all_to_all | solution.py:249
  89.3 1.0 %copy.20 = f32[8,16,8,128]{3,2,1,0:T(8,128)} copy(f32[8,16,8,128]{3,1,2,0:T(8,128)S(1)} %all_to_all.5) | data formatting | bytes 1048576 | tf_op jit(solution)/shard_map/all_to_all | solution.py:249
  (37 shorter events, 0.4 us)
Async XLA Ops:
  0.6 1.0 %copy-start.1 = (f32[64,128]{1,0:T(8,128)S(1)}, f32[64,128]{1,0:T(8,128)}, u32[]{:S(2)}) copy-start(f32[64,128]{1,0:T(8,128)} %param.10) | copy-start | bytes 98308
  2.6 7.8 %collective-permute-start = (f32[5,64,128]{2,1,0:T(8,128)S(1)}, f32[5,64,128]{2,1,0:T(8,128)S(1)}, u32[]{:S(2)}, u32[]{:S(2)}) collective-permute-start(f32[5,64,128]{2,1,0:T(8,128)S(1)} %pad_maximum_fusion.refs_2_.refs_8_), channel_id=1, source_target_pairs={{0,1},{1,0},{2,3},{3,2},{4,5},{5,4},{6,7},{7,6},{8,9},{9,8},{10,11... | collective-permute-start | bytes 491528 | tf_op jit(solution)/shard_map/ppermute | solution.py:22
  5.6 6.4 %collective-permute-start.1 = (f32[5,64,128]{2,1,0:T(8,128)S(1)}, f32[5,64,128]{2,1,0:T(8,128)S(1)}, u32[]{:S(2)}, u32[]{:S(2)}) collective-permute-start(f32[5,64,128]{2,1,0:T(8,128)S(1)} %pad_maximum_fusion.refs_2_.refs_8_), channel_id=1, source_target_pairs={{0,2},{2,0},{1,3},{3,1},{4,6},{6,4},{5,7},{7,5},{8,10},{10,8},{9,1... | collective-permute-start | bytes 491528 | tf_op jit(solution)/shard_map/ppermute | solution.py:22
  5.6 9.5 %collective-permute-start.3 = (f32[5,64,128]{2,1,0:T(8,128)S(1)}, f32[5,64,128]{2,1,0:T(8,128)S(1)}, u32[]{:S(2)}, u32[]{:S(2)}) collective-permute-start(f32[5,64,128]{2,1,0:T(8,128)S(1)} %pad_maximum_fusion.refs_2_.refs_8_), channel_id=1, source_target_pairs={{0,4},{4,8},{8,12},{12,16},{16,20},{20,24},{24,28},{28,0},{1,5},{5... | collective-permute-start | bytes 491528 | tf_op jit(solution)/shard_map/ppermute | solution.py:22
  7.1 9.8 %collective-permute-start.4 = (f32[5,64,128]{2,1,0:T(8,128)S(1)}, f32[5,64,128]{2,1,0:T(8,128)S(1)}, u32[]{:S(2)}, u32[]{:S(2)}) collective-permute-start(f32[5,64,128]{2,1,0:T(8,128)S(1)} %pad_maximum_fusion.refs_2_.refs_8_), channel_id=1, source_target_pairs={{0,28},{4,0},{8,4},{12,8},{16,12},{20,16},{24,20},{28,24},{1,29},{... | collective-permute-start | bytes 491528 | tf_op jit(solution)/shard_map/ppermute | solution.py:22
  10.4 0.7 copy-start.4
  10.4 6.6 %collective-permute-start.2 = (f32[5,64,128]{2,1,0:T(8,128)S(1)}, f32[5,64,128]{2,1,0:T(8,128)S(1)}, u32[]{:S(2)}, u32[]{:S(2)}) collective-permute-start(f32[5,64,128]{2,1,0:T(8,128)S(1)} %collective-permute-done.refs_3_.refs_9_), channel_id=1, source_target_pairs={{0,2},{2,0},{1,3},{3,1},{4,6},{6,4},{5,7},{7,5},{8,10},{10,8},{9,1... | collective-permute-start | bytes 491528 | tf_op jit(solution)/shard_map/ppermute | solution.py:22
  29.4 4.9 %collective-permute-start.6 = (f32[3,64,128]{2,1,0:T(8,128)S(1)}, f32[3,64,128]{2,1,0:T(8,128)S(1)}, u32[]{:S(2)}, u32[]{:S(2)}) collective-permute-start(f32[3,64,128]{2,1,0:T(8,128)S(1)} %get-tuple-element.17), channel_id=1, source_target_pairs={{0,2},{2,0},{1,3},{3,1},{4,6},{6,4},{5,7},{7,5},{8,10},{10,8},{9,1... | collective-permute-start | bytes 294920 | tf_op jit(solution)/shard_map/ppermute | solution.py:22
  29.5 7.9 %collective-permute-start.9 = (f32[3,64,128]{2,1,0:T(8,128)S(1)}, f32[3,64,128]{2,1,0:T(8,128)S(1)}, u32[]{:S(2)}, u32[]{:S(2)}) collective-permute-start(f32[3,64,128]{2,1,0:T(8,128)S(1)} %get-tuple-element.19), channel_id=1, source_target_pairs={{0,4},{4,8},{8,12},{12,16},{16,20},{20,24},{24,28},{28,0},{1,5},{5... | collective-permute-start | bytes 294920 | tf_op jit(solution)/shard_map/ppermute | solution.py:22
  30.1 7.4 %collective-permute-start.8 = (f32[3,64,128]{2,1,0:T(8,128)S(1)}, f32[3,64,128]{2,1,0:T(8,128)S(1)}, u32[]{:S(2)}, u32[]{:S(2)}) collective-permute-start(f32[3,64,128]{2,1,0:T(8,128)S(1)} %get-tuple-element.18), channel_id=1, source_target_pairs={{0,28},{4,0},{8,4},{12,8},{16,12},{20,16},{24,20},{28,24},{1,29},{... | collective-permute-start | bytes 294920 | tf_op jit(solution)/shard_map/ppermute | solution.py:22
  34.3 3.1 %collective-permute-start.5 = (f32[3,64,128]{2,1,0:T(8,128)S(1)}, f32[3,64,128]{2,1,0:T(8,128)S(1)}, u32[]{:S(2)}, u32[]{:S(2)}) collective-permute-start(f32[3,64,128]{2,1,0:T(8,128)S(1)} %get-tuple-element.15), channel_id=1, source_target_pairs={{0,2},{2,0},{1,3},{3,1},{4,6},{6,4},{5,7},{7,5},{8,10},{10,8},{9,1... | collective-permute-start | bytes 294920 | tf_op jit(solution)/shard_map/ppermute | solution.py:22
  34.3 5.3 %copy-start = (f32[64,3,128]{2,0,1:T(8,128)S(1)}, f32[64,3,128]{2,0,1:T(8,128)}, u32[]{:S(2)}) copy-start(f32[64,3,128]{2,0,1:T(8,128)} %param.8) | copy-start | bytes 294916
  34.3 5.3 %copy-start.2 = (f32[64,3,128]{2,0,1:T(8,128)S(1)}, f32[64,3,128]{2,0,1:T(8,128)}, u32[]{:S(2)}) copy-start(f32[64,3,128]{2,0,1:T(8,128)} %param.9) | copy-start | bytes 294916
  34.3 5.3 %collective-permute-start.7 = (f32[3,64,128]{2,1,0:T(8,128)S(1)}, f32[3,64,128]{2,1,0:T(8,128)S(1)}, u32[]{:S(2)}, u32[]{:S(2)}) collective-permute-start(f32[3,64,128]{2,1,0:T(8,128)S(1)} %add.66), channel_id=1, source_target_pairs={{0,1},{1,0},{2,3},{3,2},{4,5},{5,4},{6,7},{7,6},{8,9},{9,8},{10,11... | collective-permute-start | bytes 294920 | tf_op jit(solution)/shard_map/ppermute | solution.py:22
  39.6 5.1 %copy-start.3 = (s32[64,1]{0,1:T(1,128)S(1)}, s32[64,1]{0,1:T(1,128)}, u32[]{:S(2)}) copy-start(s32[64,1]{0,1:T(1,128)} %param.15) | copy-start | bytes 772
  39.7 5.1 %collective-permute-start.10 = (f32[3,64,128]{2,1,0:T(8,128)S(1)}, f32[3,64,128]{2,1,0:T(8,128)S(1)}, u32[]{:S(2)}, u32[]{:S(2)}) collective-permute-start(f32[3,64,128]{2,1,0:T(8,128)S(1)} %get-tuple-element.29.refs_2_), channel_id=1, source_target_pairs={{0,1},{1,0},{2,3},{3,2},{4,5},{5,4},{6,7},{7,6},{8,9},{9,8},{10,11... | collective-permute-start | bytes 294920 | tf_op jit(solution)/shard_map/ppermute | solution.py:22
  40.0 4.9 %collective-permute-start.11 = (f32[3,64,128]{2,1,0:T(8,128)S(1)}, f32[3,64,128]{2,1,0:T(8,128)S(1)}, u32[]{:S(2)}, u32[]{:S(2)}) collective-permute-start(f32[3,64,128]{2,1,0:T(8,128)S(1)} %get-tuple-element.29.refs_2_), channel_id=1, source_target_pairs={{0,2},{2,0},{1,3},{3,1},{4,6},{6,4},{5,7},{7,5},{8,10},{10,8},{9,1... | collective-permute-start | bytes 294920 | tf_op jit(solution)/shard_map/ppermute | solution.py:22
  40.0 7.9 %collective-permute-start.13 = (f32[3,64,128]{2,1,0:T(8,128)S(1)}, f32[3,64,128]{2,1,0:T(8,128)S(1)}, u32[]{:S(2)}, u32[]{:S(2)}) collective-permute-start(f32[3,64,128]{2,1,0:T(8,128)S(1)} %get-tuple-element.29.refs_2_), channel_id=1, source_target_pairs={{0,4},{4,8},{8,12},{12,16},{16,20},{20,24},{24,28},{28,0},{1,5},{5... | collective-permute-start | bytes 294920 | tf_op jit(solution)/shard_map/ppermute | solution.py:22
  40.0 7.9 %collective-permute-start.14 = (f32[3,64,128]{2,1,0:T(8,128)S(1)}, f32[3,64,128]{2,1,0:T(8,128)S(1)}, u32[]{:S(2)}, u32[]{:S(2)}) collective-permute-start(f32[3,64,128]{2,1,0:T(8,128)S(1)} %get-tuple-element.29.refs_2_), channel_id=1, source_target_pairs={{0,28},{4,0},{8,4},{12,8},{16,12},{20,16},{24,20},{28,24},{1,29},{... | collective-permute-start | bytes 294920 | tf_op jit(solution)/shard_map/ppermute | solution.py:22
  44.7 3.2 %collective-permute-start.12 = (f32[3,64,128]{2,1,0:T(8,128)S(1)}, f32[3,64,128]{2,1,0:T(8,128)S(1)}, u32[]{:S(2)}, u32[]{:S(2)}) collective-permute-start(f32[3,64,128]{2,1,0:T(8,128)S(1)} %collective-permute-done.10.refs_3_), channel_id=1, source_target_pairs={{0,2},{2,0},{1,3},{3,1},{4,6},{6,4},{5,7},{7,5},{8,10},{10,8},{9,1... | collective-permute-start | bytes 294920 | tf_op jit(solution)/shard_map/ppermute | solution.py:22
  60.4 5.0 %collective-permute-start.16 = (f32[3,64,128]{2,1,0:T(8,128)S(1)}, f32[3,64,128]{2,1,0:T(8,128)S(1)}, u32[]{:S(2)}, u32[]{:S(2)}) collective-permute-start(f32[3,64,128]{2,1,0:T(8,128)S(1)} %get-tuple-element.23), channel_id=1, source_target_pairs={{0,2},{2,0},{1,3},{3,1},{4,6},{6,4},{5,7},{7,5},{8,10},{10,8},{9,1... | collective-permute-start | bytes 294920 | tf_op jit(solution)/shard_map/ppermute | solution.py:22
  60.6 7.9 %collective-permute-start.19 = (f32[3,64,128]{2,1,0:T(8,128)S(1)}, f32[3,64,128]{2,1,0:T(8,128)S(1)}, u32[]{:S(2)}, u32[]{:S(2)}) collective-permute-start(f32[3,64,128]{2,1,0:T(8,128)S(1)} %get-tuple-element.25), channel_id=1, source_target_pairs={{0,4},{4,8},{8,12},{12,16},{16,20},{20,24},{24,28},{28,0},{1,5},{5... | collective-permute-start | bytes 294920 | tf_op jit(solution)/shard_map/ppermute | solution.py:22
  60.9 7.7 %collective-permute-start.18 = (f32[3,64,128]{2,1,0:T(8,128)S(1)}, f32[3,64,128]{2,1,0:T(8,128)S(1)}, u32[]{:S(2)}, u32[]{:S(2)}) collective-permute-start(f32[3,64,128]{2,1,0:T(8,128)S(1)} %get-tuple-element.24), channel_id=1, source_target_pairs={{0,28},{4,0},{8,4},{12,8},{16,12},{20,16},{24,20},{28,24},{1,29},{... | collective-permute-start | bytes 294920 | tf_op jit(solution)/shard_map/ppermute | solution.py:22
  65.4 3.2 %collective-permute-start.15 = (f32[3,64,128]{2,1,0:T(8,128)S(1)}, f32[3,64,128]{2,1,0:T(8,128)S(1)}, u32[]{:S(2)}, u32[]{:S(2)}) collective-permute-start(f32[3,64,128]{2,1,0:T(8,128)S(1)} %get-tuple-element.21), channel_id=1, source_target_pairs={{0,2},{2,0},{1,3},{3,1},{4,6},{6,4},{5,7},{7,5},{8,10},{10,8},{9,1... | collective-permute-start | bytes 294920 | tf_op jit(solution)/shard_map/ppermute | solution.py:22
  65.4 5.3 %collective-permute-start.17 = (f32[3,64,128]{2,1,0:T(8,128)S(1)}, f32[3,64,128]{2,1,0:T(8,128)S(1)}, u32[]{:S(2)}, u32[]{:S(2)}) collective-permute-start(f32[3,64,128]{2,1,0:T(8,128)S(1)} %add.73), channel_id=1, source_target_pairs={{0,1},{1,0},{2,3},{3,2},{4,5},{5,4},{6,7},{7,6},{8,9},{9,8},{10,11... | collective-permute-start | bytes 294920 | tf_op jit(solution)/shard_map/ppermute | solution.py:22

commit v2 on v1

v2 whole, which is shorter than its diff:
```python
import functools

import jax
import jax.numpy as jnp
from jax import lax
from jax.experimental import pallas as pl
from jax.experimental.pallas import tpu as pltpu
from jax.sharding import PartitionSpec as P


STEPS = 2

coulomb = 0.3
time_step = 0.05
middle = 2.0
feature_rows = 33
moment_rows = 9
half = 16
pair_bits = 9
pair_base = 1 << pair_bits


def shifted(value, axis, steps):
    count = lax.axis_size(axis)
    return lax.ppermute(value, axis, [(i, (i + steps) % count) for i in range(count)])


def rounded(value):
    return value.astype(jnp.bfloat16).astype(jnp.float32)


def tile_kernel(clusters, tiles, *refs):
    pairs = refs[0]
    places = refs[1:7]
    fixed = refs[7:13]
    forces = refs[13:19]
    features, moments, totals = refs[19:22]
    even, odd = refs[22:27], refs[27:32]
    live = pairs[tiles]
    width = features.shape[1]
    ones = jnp.ones((clusters, width), jnp.float32)
    none = jnp.zeros((clusters, width), jnp.float32)
    for piece in range(6):
        first = piece * clusters

        def put(row, value):
            features[pl.ds(first * feature_rows + row, clusters, stride=feature_rows), :] = value

        charge = fixed[piece][3 * clusters : 4 * clusters, :]
        square = none
        for part in range(4):
            value = places[piece][part * clusters : (part + 1) * clusters, :] - middle if part < 3 else fixed[piece][4 * clusters : 5 * clusters, :]
            square = square + value * value
            high = rounded(value)
            rest = value - high
            mid = rounded(rest)
            low = rounded(rest - mid)
            put(part, high)
            put(4 + part, mid)
            put(8 + part, high)
            put(12 + part, low)
            put(16 + part, high)
            weighed = charge * value if part < 3 else charge
            weighed_high = rounded(weighed)
            base = first * moment_rows + part
            moments[pl.ds(base, clusters, stride=moment_rows), :] = weighed_high
            moments[pl.ds(base + 4, clusters, stride=moment_rows), :] = rounded(weighed - weighed_high)
        high = rounded(square)
        rest = square - high
        mid = rounded(rest)
        for row, value in enumerate((high, mid, rounded(rest - mid), none)):
            put(20 + row, value)
            put(24 + row, ones if row < 3 else none)
            put(28 + row, value)
    totals[...] = jnp.zeros_like(totals)
    row = lax.broadcasted_iota(jnp.int32, (24, width), 0) % 4
    scale = jnp.where(row == 3, 2.0, -2.0)

    def ends(t):
        pair = pairs[jnp.minimum(t, tiles - 1)]
        return pair >> pair_bits, pair & (pair_base - 1)

    def features_of(t):
        left, right = ends(t)
        left_base = left * feature_rows
        right_base = right * feature_rows
        pair_a = features[pl.ds(left_base, 8), :]
        streamed = jnp.concatenate([pair_a, pair_a, features[pl.ds(left_base + 8, 8), :]], axis=0) * scale
        streamed = jnp.concatenate([streamed, features[pl.ds(left_base + 20, 8), :]], axis=0)
        kept = jnp.concatenate(
            [
                features[pl.ds(right_base, 8), :],
                features[pl.ds(right_base + 4, 8), :],
                features[pl.ds(right_base + 12, 8), :],
                features[pl.ds(right_base + 24, 8), :],
            ],
            axis=0,
        )
        return streamed.astype(jnp.bfloat16), kept.astype(jnp.bfloat16)

    def prepared(t):
        streamed, kept = zip(features_of(t), features_of(t + 1))
        apart = jnp.zeros_like(kept[0])
        kept = jnp.concatenate(
            [jnp.concatenate([kept[0], apart], axis=1), jnp.concatenate([apart, kept[1]], axis=1)], axis=0
        )
        return jnp.concatenate(streamed, axis=0).T, kept

    def distances(streamed, kept, squares, slot):
        square = lax.dot_general(
            streamed,
            kept,
            (((1,), (0,)), ((), ())),
            preferred_element_type=jnp.float32,
        )
        squares[slot] = square[:, :width]
        squares[slot + 1] = square[:, width:]

    def strengths(squares, kept, slot):
        inverse = lax.rsqrt(squares[slot])
        strength = inverse * inverse * inverse
        high = strength.astype(jnp.bfloat16)
        low = (strength - high.astype(jnp.float32)).astype(jnp.bfloat16)
        for ref, value in zip(kept, (high, low, high.T, low.T)):
            ref[slot] = value

    def pushes(t, kept, slot):
        left, right = ends(t)
        left_at = left * moment_rows
        right_at = right * moment_rows
        active = t < live
        both = jnp.concatenate([moments[pl.ds(left_at, 8), :], moments[pl.ds(right_at, 8), :]], axis=0)
        both = both.astype(jnp.bfloat16)
        high, low, turned_high, turned_low = [ref[slot] for ref in kept]
        turned = jnp.concatenate([turned_high, turned_low], axis=1)
        straight = jnp.concatenate([high, low], axis=1)
        on_left = jnp.dot(both, turned, preferred_element_type=jnp.float32)[8:]
        on_right = jnp.dot(both, straight, preferred_element_type=jnp.float32)[:8]
        on_left = jnp.where(active, on_left[:, :width] + on_left[:, width:], 0.0)
        on_right = jnp.where(active, on_right[:, :width] + on_right[:, width:], 0.0)
        return left_at, right_at, on_left, on_right

    def phase(number, now, other, filling=0):
        first = number * half
        ready = [prepared(first + u) for u in range(0, half, 2)]
        pushed = [] if filling else [pushes(first + u - 2 * half, now[1:], u) for u in range(half)]
        if filling != 2:
            for u in range(half):
                strengths(other[0], other[1:], u)
        for u in range(0, half, 2):
            distances(*ready[u // 2], now[0], u)
        for left_at, right_at, on_left, on_right in pushed:
            totals[pl.ds(left_at, 8), :] += on_left
            totals[pl.ds(right_at, 8), :] += on_right

    def group(g, carry):
        phase(2 * g, even, odd)
        phase(2 * g + 1, odd, even)
        return carry

    phase(0, even, odd, filling=2)
    phase(1, odd, even, filling=1)
    lax.fori_loop(1, 1 + (live + 2 * half - 1) // (2 * half), group, 0)
    for piece in range(6):
        first = piece * clusters * moment_rows

        def total(row):
            return (
                totals[pl.ds(first + row, clusters, stride=moment_rows), :]
                + totals[pl.ds(first + row + 4, clusters, stride=moment_rows), :]
            )

        charge = coulomb * fixed[piece][3 * clusters : 4 * clusters, :]
        summed = total(3)
        for part in range(3):
            forces[piece][part * clusters : (part + 1) * clusters, :] = charge * ((places[piece][part * clusters : (part + 1) * clusters, :] - middle) * summed - total(part))


def tile_forces(pairs, tiles, clusters, places, fixed):
    width = places[0].shape[1]
    smem = pl.BlockSpec(memory_space=pltpu.SMEM)
    vmem = pl.BlockSpec(memory_space=pltpu.VMEM)
    stage = [pltpu.VMEM((half, width, width), jnp.float32)] + [pltpu.VMEM((half, width, width), jnp.bfloat16)] * 4
    return pl.pallas_call(
        functools.partial(tile_kernel, clusters, tiles),
        out_shape=[jax.ShapeDtypeStruct((3 * clusters, width), jnp.float32)] * 6,
        in_specs=[smem] + [vmem] * 12,
        out_specs=[vmem] * 6,
        scratch_shapes=[
            pltpu.VMEM((6 * clusters * feature_rows, width), jnp.float32),
            pltpu.VMEM((6 * clusters * moment_rows, width), jnp.float32),
            pltpu.VMEM((6 * clusters * moment_rows, width), jnp.float32),
        ]
        + stage * 2,
        compiler_params=pltpu.CompilerParams(vmem_limit_bytes=28 << 20),
        cost_estimate=pl.CostEstimate(flops=1 << 33, bytes_accessed=1 << 22, transcendentals=1 << 22),
        name="tile_forces",
    )(pairs, *places, *fixed)


def home_kernel(clusters, lists, places, charges, types, radii, tiles, live, home):
    width = charges.shape[1]
    home[0 : 3 * clusters, :] = places[...]
    home[3 * clusters : 4 * clusters, :] = charges[...]
    radius = jnp.zeros(types.shape, jnp.float32)
    for kind in range(radii.shape[0]):
        radius = jnp.where(types[...] == kind, radii[kind], radius)
    home[4 * clusters : 5 * clusters, :] = radius
    first = 5 * clusters
    for side in range(2):
        for row in range(lists):
            part = tiles[side : side + 1, row * width : (row + 1) * width]
            home[pl.ds(first + side * lists + row, 1), :] = part.astype(jnp.float32)
    rest = home.shape[0] - first - 2 * lists
    home[pl.ds(first + 2 * lists, rest), :] = jnp.full((rest, width), live[0]).astype(jnp.float32)


def home_array(places, charges, types, radii, tiles, live):
    clusters, width = charges.shape
    lists = tiles.shape[1] // width
    extra = -(-(2 * lists + 1) // 8) * 8
    smem = pl.BlockSpec(memory_space=pltpu.SMEM)
    vmem = pl.BlockSpec(memory_space=pltpu.VMEM)
    return pl.pallas_call(
        functools.partial(home_kernel, clusters, lists),
        out_shape=jax.ShapeDtypeStruct((5 * clusters + extra, width), jnp.float32),
        in_specs=[vmem, vmem, vmem, smem, vmem, smem],
        out_specs=vmem,
        name="home_array",
    )(places, charges, types, radii, tiles, live)


def plan_kernel(clusters, lists, mine, *refs):
    pieces, plan = refs[:4], refs[4]
    width = plan.shape[1]
    tiles = lists * width
    first = 5 * clusters
    me = mine[0]
    lane = lax.broadcasted_iota(jnp.int32, (lists, width), 1)
    place = (lax.broadcasted_iota(jnp.int32, (lists, width), 0) * width + lane).astype(jnp.float32)
    source = lax.broadcasted_iota(jnp.int32, (width, width), 0)
    target = lax.broadcasted_iota(jnp.int32, (width, width), 1)
    before = jnp.where(source < target, 1.0, 0.0).astype(jnp.bfloat16)

    def ranked(mask):
        inside = jnp.dot(mask.astype(jnp.bfloat16), before, preferred_element_type=jnp.float32)
        counts = [jnp.sum(mask[row : row + 1]) for row in range(lists)]
        return inside, counts

    sides, shared, towers = [], [], []
    for piece in pieces:
        left = piece[pl.ds(first, lists), :]
        right = piece[pl.ds(first + lists, lists), :]
        used = place < piece[pl.ds(first + 2 * lists, 1), :]
        plate = jnp.maximum(left, right) < 4 * clusters
        sides.append((left, right))
        shared.append(jnp.where(used & plate, 1.0, 0.0))
        towers.append(jnp.where(used & ~plate, 1.0, 0.0))
    ranks = [ranked(mask) for mask in shared]
    plates = [sum(counts) for _, counts in ranks]
    tower_counts = [jnp.sum(mask) for mask in towers]
    total = sum(plates)

    def filled(level):
        return sum([jnp.maximum(level - count, 0.0) for count in tower_counts])

    level = jnp.float32(0.0)
    step = 1
    while step < 2 * tiles:
        step *= 2
    while step >= 1:
        level = jnp.where(filled(level + step) < total, level + step, level)
        step //= 2
    shares = [jnp.maximum(level + 1.0 - count, 0.0) for count in tower_counts]

    def ahead(values, index):
        here = me ^ index
        return sum([jnp.where((me ^ other) < here, value, 0.0) for other, value in enumerate(values)])

    begin = jnp.minimum(ahead(shares, 0), total)
    end = jnp.minimum(ahead(shares, 0) + shares[0], total)
    taken = end - begin
    slot_index = lax.broadcasted_iota(jnp.int32, (tiles, width), 0).astype(jnp.float32)
    row_index = lax.broadcasted_iota(jnp.int32, (8, width), 0)
    chosen = jnp.zeros((8, tiles), jnp.float32)
    own_inside, own_counts = ranked(towers[0])
    for index in range(4):
        inside, counts = ranks[index]
        base = ahead(plates, index)
        own_base = taken
        for row in range(lists):
            slot = inside[row : row + 1] + (base - begin)
            mine_now = (shared[index][row : row + 1] > 0.5) & (slot > -0.5) & (slot < taken - 0.5)
            slot = jnp.where(mine_now, slot, -1.0)
            base = base + counts[row]
            if index == 0:
                slot = jnp.where(towers[0][row : row + 1] > 0.5, own_inside[row : row + 1] + own_base, slot)
                own_base = own_base + own_counts[row]
            values = jnp.zeros((8, width), jnp.float32)
            for side in range(2):
                rows = sides[index][side][row : row + 1]
                block = jnp.floor((rows + 0.5) * (1.0 / clusters))
                within = rows - block * clusters
                whole = block.astype(jnp.int32)
                moved = jnp.where(whole < 4, whole ^ me, whole).astype(jnp.float32)
                values = jnp.where(row_index == 2 * side, moved, values)
                values = jnp.where(row_index == 2 * side + 1, within, values)
            hits = jnp.where(slot_index == slot, 1.0, 0.0).astype(jnp.bfloat16)
            chosen += lax.dot_general(
                values.astype(jnp.bfloat16), hits, (((1,), (1,)), ((), ())), preferred_element_type=jnp.float32
            )
    whole_row = lax.broadcasted_iota(jnp.int32, (8, tiles), 0)
    scales = (float(clusters * pair_base), float(pair_base), float(clusters), 1.0)
    scale = jnp.zeros((8, tiles), jnp.float32)
    for row, value in enumerate(scales):
        scale = jnp.where(whole_row == row, value, scale)
    packed = jnp.sum(chosen * scale, axis=0, keepdims=True).astype(jnp.int32)
    count = (taken + tower_counts[0]).astype(jnp.int32)
    for row in range(lists):
        plan[row : row + 1, :] = packed[:, row * width : (row + 1) * width]
    plan[pl.ds(lists, plan.shape[0] - lists), :] = jnp.full((plan.shape[0] - lists, width), count)


def planned(mine, clusters, tiles, pieces):
    width = pieces[0].shape[1]
    lists = tiles // width
    smem = pl.BlockSpec(memory_space=pltpu.SMEM)
    vmem = pl.BlockSpec(memory_space=pltpu.VMEM)
    plan = pl.pallas_call(
        functools.partial(plan_kernel, clusters, lists),
        out_shape=jax.ShapeDtypeStruct((-(-(lists + 1) // 8) * 8, width), jnp.int32),
        in_specs=[smem] + [vmem] * 4,
        out_specs=vmem,
        compiler_params=pltpu.CompilerParams(vmem_limit_bytes=8 << 20),
        name="plan",
    )(mine.reshape(1), *pieces)
    return plan.reshape(-1)


def imported(value):
    below = shifted(value, "gz", 1)
    above = shifted(value, "gz", -1)
    over_x = shifted(value, "gx", 1)
    over_y = shifted(value, "gy", 1)
    beyond = shifted(over_x, "gy", 1)
    return [value, over_x, over_y, beyond, below, above]


def returned(partial):
    below = shifted(partial[4], "gz", -1)
    above = shifted(partial[5], "gz", 1)
    direct = shifted(partial[2], "gy", 1)
    beyond = shifted(partial[3], "gy", 1)
    across = shifted(partial[1] + beyond, "gx", 1)
    return partial[0] + direct + across + below + above


def local(positions, velocities, charges, atom_types, type_radius, tiles, tile_live, destinations):
    clusters = positions.shape[0]
    width = positions.shape[2]
    mine = lax.axis_index("gy") * lax.axis_size("gx") + lax.axis_index("gx")
    tile_count = tiles.shape[0]
    places = jnp.transpose(positions, (1, 0, 2)).reshape(3 * clusters, width)
    moving = jnp.transpose(velocities, (1, 0, 2)).reshape(3 * clusters, width)
    home = home_array(places, charges, atom_types, type_radius, jnp.transpose(tiles), tile_live)
    steady = home[3 * clusters : 5 * clusters]
    groups = lax.axis_size("gz")
    capacity = max(2, 2 * clusters // groups)
    slot_count = groups * capacity
    target_ids = destinations[:, 0]
    onehot = (target_ids[:, None] == jnp.arange(groups, dtype=jnp.int32)[None, :]).astype(jnp.int32)
    rank_before = jnp.cumsum(onehot, axis=0) - onehot
    position = jnp.sum(rank_before * onehot, axis=1) + target_ids * capacity
    select = (position[None, :] == jnp.arange(slot_count, dtype=jnp.int32)[:, None]).astype(jnp.float32)

    def migrated(channels):
        count = channels.shape[0] // clusters
        channels = channels.reshape(count, clusters, width)
        slots = jnp.einsum("sc,fca->fsa", select, channels, precision=lax.Precision.HIGHEST)
        slots = jnp.transpose(slots.reshape(count, groups, capacity, width), (1, 0, 2, 3))
        received = lax.all_to_all(slots, "gz", split_axis=0, concat_axis=0, tiled=True)
        return jnp.transpose(received, (1, 0, 2, 3)).reshape(count, slot_count, width)

    fixed = imported(home)
    pairs = planned(mine, clusters, tile_count, fixed[:4])
    current = fixed
    for step_index in range(STEPS):
        if step_index:
            current = imported(places)
            sent = migrated(jnp.concatenate([places, moving, steady], axis=0))
        forces = returned(tile_forces(pairs, tile_count, clusters, current, fixed))
        if not step_index:
            moving = moving + time_step * forces
            places = places + time_step * moving
    pushed = migrated(forces)
    moved = sent[3:6] + time_step * pushed
    placed = sent[0:3] + time_step * moved
    arrived = jnp.concatenate([placed, moved, sent[6:]], axis=0)
    return (jnp.transpose(forces.reshape(3, clusters, width), (1, 0, 2)), jnp.transpose(arrived, (1, 0, 2)))


def solution(mesh):
    whole = ("gz", "gy", "gx")
    placed = (
        P(whole, None, None),
        P(whole, None, None),
        P(whole, None),
        P(whole, None),
        P(),
        P(whole, None),
        P(whole),
        P(whole, None),
    )
    return jax.shard_map(
        local,
        mesh=mesh,
        in_specs=placed,
        out_specs=(P(whole, None, None), P(whole, None, None)),
        check_vma=False,
    )
```

time: 90.7 us -> 79.3 us (0.87)
  blocking collectives: 17.4 us -> 0 us
  starting transfers between devices: 22.7 us -> 33.4 us
  Pallas kernels: 24.9 us -> 17.3 us
  local copies, waits for them, and re-layouts: 1.93 us -> 4.51 us
  waiting for transfers between devices: 18.3 us -> 20.8 us
  other arithmetic: 3.03 us -> 0.57 us
    all_to_all x1 -> x0, blocking collectives: 17.4 us -> none  [local(): lax.all_to_all(sent_slots.reshape(groups, capacity, 8, width), 'gz', spli...]
    all_to_all x0 -> x2, waiting for transfers between devices: none -> 7.73 us  [migrated(): lax.all_to_all(slots, 'gz', split_axis=0, concat_axis=0, tiled=True)]
    pallas_call x2 -> x4, Pallas kernels: 24.9 us -> 17.3 us  [the longest x2 15.1 us: tile_forces(): pl.pallas_call(functools.partial(tile_kernel, clusters, tiles), out_shape...]
    all_to_all x0 -> x2, starting transfers between devices: none -> 7.16 us  [migrated(): lax.all_to_all(slots, 'gz', split_axis=0, concat_axis=0, tiled=True)]
    ppermute x20, waiting for transfers between devices: 18.3 us -> 13.1 us  [shifted(): lax.ppermute(value, axis, [(i, (i + steps) % count) for i in range(count)])]
    ppermute x20, starting transfers between devices: 22.7 us -> 26.2 us  [shifted(): lax.ppermute(value, axis, [(i, (i + steps) % count) for i in range(count)])]
    unnamed x10 -> x13, local copies, waits for them, and re-layouts: 0.66 us -> 2.92 us
    reshape x2, local copies, waits for them, and re-layouts: 0.18 us -> 1.54 us  [migrated(): slots.reshape(count, groups, capacity, width)]
  transfers between devices with their start and end apart: 20 -> 22, of which waited for: 7 -> 9; matrix products, arithmetic and copies ran while one was open for 1% -> 4% of each run, Pallas kernels for 0% -> 10%
where the time goes in v2:
time: 79.3 us; the launch traced here: 78.9 us
  starting transfers between devices  33.4 us (42%)
  waiting for transfers between devices  20.8 us (26%)
  Pallas kernels  17.3 us (22%)
  local copies, waits for them, and re-layouts  4.51 us (6%)
  between operations  1.48 us (2%)
  matrix products  0.84 us (1%)
    ppermute x20, starting transfers between devices, shifted(): lax.ppermute(value, axis, [(i, (i + steps) % count) for i in range(count)])  26.2 us
    pallas_call x2, Pallas kernels, tile_forces(): pl.pallas_call(functools.partial(tile_kernel, clusters, tiles), out_shape...  15.1 us
    ppermute x20, waiting for transfers between devices, shifted(): lax.ppermute(value, axis, [(i, (i + steps) % count) for i in range(count)])  13.1 us
    all_to_all x2, waiting for transfers between devices, migrated(): lax.all_to_all(slots, 'gz', split_axis=0, concat_axis=0, tiled=True)  7.73 us
    all_to_all x2, starting transfers between devices, migrated(): lax.all_to_all(slots, 'gz', split_axis=0, concat_axis=0, tiled=True)  7.16 us
    unnamed x13, local copies, waits for them, and re-layouts  2.92 us
    pallas_call x1, Pallas kernels, home_array(): pl.pallas_call(functools.partial(home_kernel, clusters, lists), out_shape...  1.64 us
  transfers between devices with their start and end apart: 22, of which 9 were waited for; matrix products, arithmetic and copies ran while one was open for 4% of the time, Pallas kernels for 10%

profile of v2, /device:TPU:0, one launch (start us, length us, event | category | flops | bytes accessed | tf_op | source)
XLA Modules:
  0.0 78.9 jit_solution(5061978682000032224)
XLA Ops:
  1.3 1.6 %home_array.1.refs_0_.refs_1_.refs_7_ = f32[328,128]{1,0:T(8,128)} custom-call(f32[192,128]{1,0:T(8,128)} %bitcast.57, f32[64,128]{1,0:T(8,128)} %charges.1, s32[64,128]{1,0:T(8,128)} %types.1, f32[16]{0:T(128)} %radii.1, s32[2,256]{1,0:T(2,128)} %bitcast.60, s32[1]{0:T(128)S(6)} %copy.29.live), custom_call_target="tpu_custom_call" | custom-call | tf_op jit(solution)/shard_map/home_array/pallas_call | solution.py:224
  2.9 3.0 %collective-permute-start = (f32[328,128]{1,0:T(8,128)}, f32[328,128]{1,0:T(8,128)S(1)}, u32[]{:S(2)}, u32[]{:S(2)}) collective-permute-start(f32[328,128]{1,0:T(8,128)} %home_array.1.refs_0_.refs_1_.refs_7_), channel_id=1, source_target_pairs={{0,1},{1,0},{2,3},{3,2},{4,5},{5,4},{6,7},{7,6},{8,9},{9,8},{10,11... | collective-permute-start | bytes 503816 | tf_op jit(solution)/shard_map/ppermute | solution.py:25
  5.9 1.5 %collective-permute-start.3 = (f32[328,128]{1,0:T(8,128)}, f32[328,128]{1,0:T(8,128)S(1)}, u32[]{:S(2)}, u32[]{:S(2)}) collective-permute-start(f32[328,128]{1,0:T(8,128)} %home_array.1.refs_0_.refs_1_.refs_7_), channel_id=1, source_target_pairs={{0,4},{4,8},{8,12},{12,16},{16,20},{20,24},{24,28},{28,0},{1,5},{5... | collective-permute-start | bytes 503816 | tf_op jit(solution)/shard_map/ppermute | solution.py:25
  7.4 3.2 %collective-permute-start.4 = (f32[328,128]{1,0:T(8,128)}, f32[328,128]{1,0:T(8,128)S(1)}, u32[]{:S(2)}, u32[]{:S(2)}) collective-permute-start(f32[328,128]{1,0:T(8,128)} %home_array.1.refs_0_.refs_1_.refs_7_), channel_id=1, source_target_pairs={{0,28},{4,0},{8,4},{12,8},{16,12},{20,16},{24,20},{28,24},{1,29},{... | collective-permute-start | bytes 503816 | tf_op jit(solution)/shard_map/ppermute | solution.py:25
  10.7 0.6 copy-done.5
  11.5 0.6 collective-permute-done.2.refs_3_.refs_4_.refs_10_
  12.1 0.9 %copy-done = f32[328,128]{1,0:T(8,128)S(1)} copy-done((f32[328,128]{1,0:T(8,128)S(1)}, f32[328,128]{1,0:T(8,128)}, u32[]{:S(2)}) %copy-start) | copy-done | bytes 167960
  13.0 0.5 plan.1
  13.5 2.2 %collective-permute-done.3.refs_5_.refs_11_ = f32[328,128]{1,0:T(8,128)S(1)} collective-permute-done((f32[328,128]{1,0:T(8,128)}, f32[328,128]{1,0:T(8,128)S(1)}, u32[]{:S(2)}, u32[]{:S(2)}) %collective-permute-start.3) | collective-permute-done | bytes 167968 | tf_op jit(solution)/shard_map/ppermute | solution.py:25
  15.7 1.9 %collective-permute-done.4.refs_6_.refs_12_ = f32[328,128]{1,0:T(8,128)S(1)} collective-permute-done((f32[328,128]{1,0:T(8,128)}, f32[328,128]{1,0:T(8,128)S(1)}, u32[]{:S(2)}, u32[]{:S(2)}) %collective-permute-start.4) | collective-permute-done | bytes 167968 | tf_op jit(solution)/shard_map/ppermute | solution.py:25
  17.6 7.6 %tile_forces.2 = (f32[192,128]{1,0:T(8,128)S(1)}, f32[192,128]{1,0:T(8,128)S(1)}, f32[192,128]{1,0:T(8,128)S(1)}, f32[192,128]{1,0:T(8,128)S(1)}, f32[192,128]{1,0:T(8,128)S(1)}, /*index=5*/f32[192,128]{1,0:T(8,128)S(1)}) custom-call(s32[1024]{0:T(1024)S(1)} %bitcast.48, f32[328,128]{1,0:T(8,128)S(1)} %copy-done.1, ...), custom_call_target="tpu_custom_call" | custom-call | flops 8589934592 | bytes 4194304 | tf_op jit(solution)/shard_map/tile_forces/pallas_call | solution.py:184
  25.8 4.5 %collective-permute-start.8 = (f32[192,128]{1,0:T(8,128)S(1)}, f32[192,128]{1,0:T(8,128)S(1)}, u32[]{:S(2)}, u32[]{:S(2)}) collective-permute-start(f32[192,128]{1,0:T(8,128)S(1)} %get-tuple-element.18), channel_id=1, source_target_pairs={{0,28},{4,0},{8,4},{12,8},{16,12},{20,16},{24,20},{28,24},{1,29},{... | collective-permute-start | bytes 294920 | tf_op jit(solution)/shard_map/ppermute | solution.py:25
  30.3 0.6 collective-permute-start.7
  30.9 2.6 %collective-permute-done.9 = f32[192,128]{1,0:T(8,128)S(1)} collective-permute-done((f32[192,128]{1,0:T(8,128)S(1)}, f32[192,128]{1,0:T(8,128)S(1)}, u32[]{:S(2)}, u32[]{:S(2)}) %collective-permute-start.9) | collective-permute-done | bytes 98336 | tf_op jit(solution)/shard_map/ppermute | solution.py:25
  33.5 2.0 %collective-permute-done.8 = f32[192,128]{1,0:T(8,128)S(1)} collective-permute-done((f32[192,128]{1,0:T(8,128)S(1)}, f32[192,128]{1,0:T(8,128)S(1)}, u32[]{:S(2)}, u32[]{:S(2)}) %collective-permute-start.8) | collective-permute-done | bytes 98336 | tf_op jit(solution)/shard_map/ppermute | solution.py:25
  35.6 0.6 collective-permute-start.10
  36.2 0.8 collective-permute-start.13
  36.9 4.0 %collective-permute-start.14 = (f32[192,128]{1,0:T(8,128)S(1)}, f32[192,128]{1,0:T(8,128)S(1)}, u32[]{:S(2)}, u32[]{:S(2)}) collective-permute-start(f32[192,128]{1,0:T(8,128)S(1)} %get-tuple-element.28.refs_1_), channel_id=1, source_target_pairs={{0,28},{4,0},{8,4},{12,8},{16,12},{20,16},{24,20},{28,24},{1,29},{... | collective-permute-start | bytes 294920 | tf_op jit(solution)/shard_map/ppermute | solution.py:25
  41.0 0.5 fusion.4
  41.5 0.8 %copy.27 = f32[8,8,16,128]{3,2,0,1:T(8,128)} copy(f32[8,8,16,128]{3,2,1,0:T(8,128)S(1)} %bitcast.52) | data formatting | bytes 1048576 | tf_op jit(solution)/shard_map/reshape | solution.py:380
  42.3 3.5 %all-to-all-start = ((f32[8,8,16,128]{3,2,1,0:T(8,128)}), f32[8,8,16,128]{3,2,1,0:T(8,128)S(1)}, u32[]{:S(2)}, u32[]{:S(2)}) async-start(f32[8,8,16,128]{3,2,1,0:T(8,128)} %bitcast.46), calls=%async_computation | async-start | bytes 1048576 | tf_op jit(solution)/shard_map/all_to_all | solution.py:381
  45.9 7.6 %tile_forces.3 = (f32[192,128]{1,0:T(8,128)S(1)}, f32[192,128]{1,0:T(8,128)S(1)}, f32[192,128]{1,0:T(8,128)S(1)}, f32[192,128]{1,0:T(8,128)S(1)}, f32[192,128]{1,0:T(8,128)S(1)}, /*index=5*/f32[192,128]{1,0:T(8,128)S(1)}) custom-call(s32[1024]{0:T(1024)S(1)} %bitcast.49, f32[192,128]{1,0:T(8,128)S(1)} %get-tuple-element.28.refs_1_, ...), custom_call_target="tpu_custom_call" | custom-call | flops 8589934592 | bytes 4194304 | tf_op jit(solution)/shard_map/tile_forces/pallas_call | solution.py:184
  53.5 0.6 collective-permute-start.16
  54.0 1.7 %collective-permute-start.19 = (f32[192,128]{1,0:T(8,128)S(1)}, f32[192,128]{1,0:T(8,128)S(1)}, u32[]{:S(2)}, u32[]{:S(2)}) collective-permute-start(f32[192,128]{1,0:T(8,128)S(1)} %get-tuple-element.25), channel_id=1, source_target_pairs={{0,4},{4,8},{8,12},{12,16},{16,20},{20,24},{24,28},{28,0},{1,5},{5... | collective-permute-start | bytes 294920 | tf_op jit(solution)/shard_map/ppermute | solution.py:25
  55.7 3.9 %collective-permute-start.18 = (f32[192,128]{1,0:T(8,128)S(1)}, f32[192,128]{1,0:T(8,128)S(1)}, u32[]{:S(2)}, u32[]{:S(2)}) collective-permute-start(f32[192,128]{1,0:T(8,128)S(1)} %get-tuple-element.24), channel_id=1, source_target_pairs={{0,28},{4,0},{8,4},{12,8},{16,12},{20,16},{24,20},{28,24},{1,29},{... | collective-permute-start | bytes 294920 | tf_op jit(solution)/shard_map/ppermute | solution.py:25
  59.6 1.6 %collective-permute-start.17 = (f32[192,128]{1,0:T(8,128)S(1)}, f32[192,128]{1,0:T(8,128)S(1)}, u32[]{:S(2)}, u32[]{:S(2)}) collective-permute-start(f32[192,128]{1,0:T(8,128)S(1)} %add.64), channel_id=1, source_target_pairs={{0,1},{1,0},{2,3},{3,2},{4,5},{5,4},{6,7},{7,6},{8,9},{9,8},{10,11... | collective-permute-start | bytes 294920 | tf_op jit(solution)/shard_map/ppermute | solution.py:25
  61.2 1.7 %collective-permute-done.19 = f32[192,128]{1,0:T(8,128)S(1)} collective-permute-done((f32[192,128]{1,0:T(8,128)S(1)}, f32[192,128]{1,0:T(8,128)S(1)}, u32[]{:S(2)}, u32[]{:S(2)}) %collective-permute-start.19) | collective-permute-done | bytes 98336 | tf_op jit(solution)/shard_map/ppermute | solution.py:25
  62.9 1.6 %collective-permute-done.18 = f32[192,128]{1,0:T(8,128)S(1)} collective-permute-done((f32[192,128]{1,0:T(8,128)S(1)}, f32[192,128]{1,0:T(8,128)S(1)}, u32[]{:S(2)}, u32[]{:S(2)}) %collective-permute-start.18) | collective-permute-done | bytes 98336 | tf_op jit(solution)/shard_map/ppermute | solution.py:25
  65.5 0.7 copy.28
  66.2 3.7 %all-to-all-start.1 = ((f32[8,3,16,128]{3,2,1,0:T(8,128)}), f32[8,3,16,128]{3,2,1,0:T(8,128)S(1)}, u32[]{:S(2)}, u32[]{:S(2)}) async-start(f32[8,3,16,128]{3,2,1,0:T(8,128)} %bitcast.47), calls=%async_computation.1 | async-start | bytes 393216 | tf_op jit(solution)/shard_map/all_to_all | solution.py:381
  70.0 7.7 %all-to-all-done.1 = f32[8,3,16,128]{3,2,1,0:T(8,128)S(1)} async-done(((f32[8,3,16,128]{3,2,1,0:T(8,128)}), f32[8,3,16,128]{3,2,1,0:T(8,128)S(1)}, u32[]{:S(2)}, u32[]{:S(2)}) %all-to-all-start.1) | async-done | bytes 196640 | tf_op jit(solution)/shard_map/all_to_all | solution.py:381
  77.8 1.1 %copy.19 = f32[128,8,128]{2,1,0:T(8,128)} copy(f32[128,8,128]{2,0,1:T(8,128)S(1)} %maximum_bitcast_fusion) | data formatting | bytes 1048576
  (48 shorter events, 2.2 us)
Async XLA Ops:
  2.9 7.7 %collective-permute-start = (f32[328,128]{1,0:T(8,128)}, f32[328,128]{1,0:T(8,128)S(1)}, u32[]{:S(2)}, u32[]{:S(2)}) collective-permute-start(f32[328,128]{1,0:T(8,128)} %home_array.1.refs_0_.refs_1_.refs_7_), channel_id=1, source_target_pairs={{0,1},{1,0},{2,3},{3,2},{4,5},{5,4},{6,7},{7,6},{8,9},{9,8},{10,11... | collective-permute-start | bytes 503816 | tf_op jit(solution)/shard_map/ppermute | solution.py:25
  5.9 5.6 %collective-permute-start.1 = (f32[328,128]{1,0:T(8,128)}, f32[328,128]{1,0:T(8,128)S(1)}, u32[]{:S(2)}, u32[]{:S(2)}) collective-permute-start(f32[328,128]{1,0:T(8,128)} %home_array.1.refs_0_.refs_1_.refs_7_), channel_id=1, source_target_pairs={{0,2},{2,0},{1,3},{3,1},{4,6},{6,4},{5,7},{7,5},{8,10},{10,8},{9,1... | collective-permute-start | bytes 503816 | tf_op jit(solution)/shard_map/ppermute | solution.py:25
  5.9 9.8 %collective-permute-start.3 = (f32[328,128]{1,0:T(8,128)}, f32[328,128]{1,0:T(8,128)S(1)}, u32[]{:S(2)}, u32[]{:S(2)}) collective-permute-start(f32[328,128]{1,0:T(8,128)} %home_array.1.refs_0_.refs_1_.refs_7_), channel_id=1, source_target_pairs={{0,4},{4,8},{8,12},{12,16},{16,20},{20,24},{24,28},{28,0},{1,5},{5... | collective-permute-start | bytes 503816 | tf_op jit(solution)/shard_map/ppermute | solution.py:25
  7.4 10.2 %collective-permute-start.4 = (f32[328,128]{1,0:T(8,128)}, f32[328,128]{1,0:T(8,128)S(1)}, u32[]{:S(2)}, u32[]{:S(2)}) collective-permute-start(f32[328,128]{1,0:T(8,128)} %home_array.1.refs_0_.refs_1_.refs_7_), channel_id=1, source_target_pairs={{0,28},{4,0},{8,4},{12,8},{16,12},{20,16},{24,20},{28,24},{1,29},{... | collective-permute-start | bytes 503816 | tf_op jit(solution)/shard_map/ppermute | solution.py:25
  10.6 0.7 copy-start.5
  10.6 1.4 %collective-permute-start.2 = (f32[328,128]{1,0:T(8,128)S(1)}, f32[328,128]{1,0:T(8,128)S(1)}, u32[]{:S(2)}, u32[]{:S(2)}) collective-permute-start(f32[328,128]{1,0:T(8,128)S(1)} %collective-permute-done.refs_1_.refs_2_.refs_8_), channel_id=1, source_target_pairs={{0,2},{2,0},{1,3},{3,1},{4,6},{6,4},{5,7},{7,5},{8,10},{10,8},{9,1... | collective-permute-start | bytes 503816 | tf_op jit(solution)/shard_map/ppermute | solution.py:25
  12.0 0.9 %copy-start = (f32[328,128]{1,0:T(8,128)S(1)}, f32[328,128]{1,0:T(8,128)}, u32[]{:S(2)}) copy-start(f32[328,128]{1,0:T(8,128)} %home_array.1.refs_0_.refs_1_.refs_7_) | copy-start | bytes 503812
  13.0 4.7 %copy-start.1 = (f32[328,128]{1,0:T(8,128)S(1)}, f32[328,128]{1,0:T(8,128)}, u32[]{:S(2)}) copy-start(f32[328,128]{1,0:T(8,128)} %home_array.1.refs_0_.refs_1_.refs_7_) | copy-start | bytes 503812
  25.2 5.0 %collective-permute-start.6 = (f32[192,128]{1,0:T(8,128)S(1)}, f32[192,128]{1,0:T(8,128)S(1)}, u32[]{:S(2)}, u32[]{:S(2)}) collective-permute-start(f32[192,128]{1,0:T(8,128)S(1)} %get-tuple-element.17), channel_id=1, source_target_pairs={{0,2},{2,0},{1,3},{3,1},{4,6},{6,4},{5,7},{7,5},{8,10},{10,8},{9,1... | collective-permute-start | bytes 294920 | tf_op jit(solution)/shard_map/ppermute | solution.py:25
  25.5 8.0 %collective-permute-start.9 = (f32[192,128]{1,0:T(8,128)S(1)}, f32[192,128]{1,0:T(8,128)S(1)}, u32[]{:S(2)}, u32[]{:S(2)}) collective-permute-start(f32[192,128]{1,0:T(8,128)S(1)} %get-tuple-element.19), channel_id=1, source_target_pairs={{0,4},{4,8},{8,12},{12,16},{16,20},{20,24},{24,28},{28,0},{1,5},{5... | collective-permute-start | bytes 294920 | tf_op jit(solution)/shard_map/ppermute | solution.py:25
  25.8 9.7 %collective-permute-start.8 = (f32[192,128]{1,0:T(8,128)S(1)}, f32[192,128]{1,0:T(8,128)S(1)}, u32[]{:S(2)}, u32[]{:S(2)}) collective-permute-start(f32[192,128]{1,0:T(8,128)S(1)} %get-tuple-element.18), channel_id=1, source_target_pairs={{0,28},{4,0},{8,4},{12,8},{16,12},{20,16},{24,20},{28,24},{1,29},{... | collective-permute-start | bytes 294920 | tf_op jit(solution)/shard_map/ppermute | solution.py:25
  30.2 5.3 %collective-permute-start.5 = (f32[192,128]{1,0:T(8,128)S(1)}, f32[192,128]{1,0:T(8,128)S(1)}, u32[]{:S(2)}, u32[]{:S(2)}) collective-permute-start(f32[192,128]{1,0:T(8,128)S(1)} %get-tuple-element.15), channel_id=1, source_target_pairs={{0,2},{2,0},{1,3},{3,1},{4,6},{6,4},{5,7},{7,5},{8,10},{10,8},{9,1... | collective-permute-start | bytes 294920 | tf_op jit(solution)/shard_map/ppermute | solution.py:25
  30.2 5.3 %copy-start.4 = (f32[64,3,128]{2,0,1:T(8,128)S(1)}, f32[64,3,128]{2,0,1:T(8,128)}, u32[]{:S(2)}) copy-start(f32[64,3,128]{2,0,1:T(8,128)} %param.9) | copy-start | bytes 294916
  30.3 5.3 %copy-start.2 = (f32[64,3,128]{2,0,1:T(8,128)S(1)}, f32[64,3,128]{2,0,1:T(8,128)}, u32[]{:S(2)}) copy-start(f32[64,3,128]{2,0,1:T(8,128)} %param.8) | copy-start | bytes 294916
  30.3 5.3 %collective-permute-start.7 = (f32[192,128]{1,0:T(8,128)S(1)}, f32[192,128]{1,0:T(8,128)S(1)}, u32[]{:S(2)}, u32[]{:S(2)}) collective-permute-start(f32[192,128]{1,0:T(8,128)S(1)} %add.57), channel_id=1, source_target_pairs={{0,1},{1,0},{2,3},{3,2},{4,5},{5,4},{6,7},{7,6},{8,9},{9,8},{10,11... | collective-permute-start | bytes 294920 | tf_op jit(solution)/shard_map/ppermute | solution.py:25
  35.6 5.3 %collective-permute-start.10 = (f32[192,128]{1,0:T(8,128)S(1)}, f32[192,128]{1,0:T(8,128)S(1)}, u32[]{:S(2)}, u32[]{:S(2)}) collective-permute-start(f32[192,128]{1,0:T(8,128)S(1)} %get-tuple-element.28.refs_1_), channel_id=1, source_target_pairs={{0,1},{1,0},{2,3},{3,2},{4,5},{5,4},{6,7},{7,6},{8,9},{9,8},{10,11... | collective-permute-start | bytes 294920 | tf_op jit(solution)/shard_map/ppermute | solution.py:25
  36.2 9.7 %collective-permute-start.11 = (f32[192,128]{1,0:T(8,128)S(1)}, f32[192,128]{1,0:T(8,128)S(1)}, u32[]{:S(2)}, u32[]{:S(2)}) collective-permute-start(f32[192,128]{1,0:T(8,128)S(1)} %get-tuple-element.28.refs_1_), channel_id=1, source_target_pairs={{0,2},{2,0},{1,3},{3,1},{4,6},{6,4},{5,7},{7,5},{8,10},{10,8},{9,1... | collective-permute-start | bytes 294920 | tf_op jit(solution)/shard_map/ppermute | solution.py:25
  36.2 9.7 %collective-permute-start.13 = (f32[192,128]{1,0:T(8,128)S(1)}, f32[192,128]{1,0:T(8,128)S(1)}, u32[]{:S(2)}, u32[]{:S(2)}) collective-permute-start(f32[192,128]{1,0:T(8,128)S(1)} %get-tuple-element.28.refs_1_), channel_id=1, source_target_pairs={{0,4},{4,8},{8,12},{12,16},{16,20},{20,24},{24,28},{28,0},{1,5},{5... | collective-permute-start | bytes 294920 | tf_op jit(solution)/shard_map/ppermute | solution.py:25
  36.9 8.9 %collective-permute-start.14 = (f32[192,128]{1,0:T(8,128)S(1)}, f32[192,128]{1,0:T(8,128)S(1)}, u32[]{:S(2)}, u32[]{:S(2)}) collective-permute-start(f32[192,128]{1,0:T(8,128)S(1)} %get-tuple-element.28.refs_1_), channel_id=1, source_target_pairs={{0,28},{4,0},{8,4},{12,8},{16,12},{20,16},{24,20},{28,24},{1,29},{... | collective-permute-start | bytes 294920 | tf_op jit(solution)/shard_map/ppermute | solution.py:25
  40.9 4.9 %collective-permute-start.12 = (f32[192,128]{1,0:T(8,128)S(1)}, f32[192,128]{1,0:T(8,128)S(1)}, u32[]{:S(2)}, u32[]{:S(2)}) collective-permute-start(f32[192,128]{1,0:T(8,128)S(1)} %collective-permute-done.10.refs_2_), channel_id=1, source_target_pairs={{0,2},{2,0},{1,3},{3,1},{4,6},{6,4},{5,7},{7,5},{8,10},{10,8},{9,1... | collective-permute-start | bytes 294920 | tf_op jit(solution)/shard_map/ppermute | solution.py:25
  42.3 23.9 %all-to-all-start = ((f32[8,8,16,128]{3,2,1,0:T(8,128)}), f32[8,8,16,128]{3,2,1,0:T(8,128)S(1)}, u32[]{:S(2)}, u32[]{:S(2)}) async-start(f32[8,8,16,128]{3,2,1,0:T(8,128)} %bitcast.46), calls=%async_computation | async-start | bytes 1048576 | tf_op jit(solution)/shard_map/all_to_all | solution.py:381
  53.5 6.1 %collective-permute-start.16 = (f32[192,128]{1,0:T(8,128)S(1)}, f32[192,128]{1,0:T(8,128)S(1)}, u32[]{:S(2)}, u32[]{:S(2)}) collective-permute-start(f32[192,128]{1,0:T(8,128)S(1)} %get-tuple-element.23), channel_id=1, source_target_pairs={{0,2},{2,0},{1,3},{3,1},{4,6},{6,4},{5,7},{7,5},{8,10},{10,8},{9,1... | collective-permute-start | bytes 294920 | tf_op jit(solution)/shard_map/ppermute | solution.py:25
  54.0 8.8 %collective-permute-start.19 = (f32[192,128]{1,0:T(8,128)S(1)}, f32[192,128]{1,0:T(8,128)S(1)}, u32[]{:S(2)}, u32[]{:S(2)}) collective-permute-start(f32[192,128]{1,0:T(8,128)S(1)} %get-tuple-element.25), channel_id=1, source_target_pairs={{0,4},{4,8},{8,12},{12,16},{16,20},{20,24},{24,28},{28,0},{1,5},{5... | collective-permute-start | bytes 294920 | tf_op jit(solution)/shard_map/ppermute | solution.py:25
  55.7 8.8 %collective-permute-start.18 = (f32[192,128]{1,0:T(8,128)S(1)}, f32[192,128]{1,0:T(8,128)S(1)}, u32[]{:S(2)}, u32[]{:S(2)}) collective-permute-start(f32[192,128]{1,0:T(8,128)S(1)} %get-tuple-element.24), channel_id=1, source_target_pairs={{0,28},{4,0},{8,4},{12,8},{16,12},{20,16},{24,20},{28,24},{1,29},{... | collective-permute-start | bytes 294920 | tf_op jit(solution)/shard_map/ppermute | solution.py:25
  59.5 4.9 %collective-permute-start.15 = (f32[192,128]{1,0:T(8,128)S(1)}, f32[192,128]{1,0:T(8,128)S(1)}, u32[]{:S(2)}, u32[]{:S(2)}) collective-permute-start(f32[192,128]{1,0:T(8,128)S(1)} %get-tuple-element.21), channel_id=1, source_target_pairs={{0,2},{2,0},{1,3},{3,1},{4,6},{6,4},{5,7},{7,5},{8,10},{10,8},{9,1... | collective-permute-start | bytes 294920 | tf_op jit(solution)/shard_map/ppermute | solution.py:25
  59.6 5.3 %collective-permute-start.17 = (f32[192,128]{1,0:T(8,128)S(1)}, f32[192,128]{1,0:T(8,128)S(1)}, u32[]{:S(2)}, u32[]{:S(2)}) collective-permute-start(f32[192,128]{1,0:T(8,128)S(1)} %add.64), channel_id=1, source_target_pairs={{0,1},{1,0},{2,3},{3,2},{4,5},{5,4},{6,7},{7,6},{8,9},{9,8},{10,11... | collective-permute-start | bytes 294920 | tf_op jit(solution)/shard_map/ppermute | solution.py:25
  64.9 0.6 copy-start.3
  66.2 11.5 %all-to-all-start.1 = ((f32[8,3,16,128]{3,2,1,0:T(8,128)}), f32[8,3,16,128]{3,2,1,0:T(8,128)S(1)}, u32[]{:S(2)}, u32[]{:S(2)}) async-start(f32[8,3,16,128]{3,2,1,0:T(8,128)} %bitcast.47), calls=%async_computation.1 | async-start | bytes 393216 | tf_op jit(solution)/shard_map/all_to_all | solution.py:381

commit v3 on v2

--- a/solution.py
+++ b/solution.py
@@ -13,6 +13,7 @@
 coulomb = 0.3
 time_step = 0.05
 middle = 2.0
+least_square = 0.3599
 feature_rows = 33
 moment_rows = 9
 half = 16
@@ -117,7 +118,7 @@
         squares[slot + 1] = square[:, width:]
 
     def strengths(squares, kept, slot):
-        inverse = lax.rsqrt(squares[slot])
+        inverse = lax.rsqrt(jnp.maximum(squares[slot], least_square))
         strength = inverse * inverse * inverse
         high = strength.astype(jnp.bfloat16)
         low = (strength - high.astype(jnp.float32)).astype(jnp.bfloat16)
@@ -235,7 +236,7 @@
     width = plan.shape[1]
     tiles = lists * width
     first = 5 * clusters
-    me = mine[0]
+    me, flip = mine[0], mine[1]
     lane = lax.broadcasted_iota(jnp.int32, (lists, width), 1)
     place = (lax.broadcasted_iota(jnp.int32, (lists, width), 0) * width + lane).astype(jnp.float32)
     source = lax.broadcasted_iota(jnp.int32, (width, width), 0)
@@ -302,7 +303,7 @@
                 block = jnp.floor((rows + 0.5) * (1.0 / clusters))
                 within = rows - block * clusters
                 whole = block.astype(jnp.int32)
-                moved = jnp.where(whole < 4, whole ^ me, whole).astype(jnp.float32)
+                moved = jnp.where(whole < 4, whole ^ me, whole ^ flip).astype(jnp.float32)
                 values = jnp.where(row_index == 2 * side, moved, values)
                 values = jnp.where(row_index == 2 * side + 1, within, values)
             hits = jnp.where(slot_index == slot, 1.0, 0.0).astype(jnp.bfloat16)
@@ -333,13 +334,21 @@
         out_specs=vmem,
         compiler_params=pltpu.CompilerParams(vmem_limit_bytes=8 << 20),
         name="plan",
-    )(mine.reshape(1), *pieces)
+    )(mine, *pieces)
     return plan.reshape(-1)
 
 
+def paired(value, first):
+    count = lax.axis_size("gz")
+    pairs = []
+    for low in range(first, count, 2):
+        pairs += [(low, (low + 1) % count), ((low + 1) % count, low)]
+    return lax.ppermute(value, "gz", pairs)
+
+
 def imported(value):
-    below = shifted(value, "gz", 1)
-    above = shifted(value, "gz", -1)
+    below = paired(value, 0)
+    above = paired(value, 1)
     over_x = shifted(value, "gx", 1)
     over_y = shifted(value, "gy", 1)
     beyond = shifted(over_x, "gy", 1)
@@ -347,8 +356,8 @@
 
 
 def returned(partial):
-    below = shifted(partial[4], "gz", -1)
-    above = shifted(partial[5], "gz", 1)
+    below = paired(partial[4], 0)
+    above = paired(partial[5], 1)
     direct = shifted(partial[2], "gy", 1)
     beyond = shifted(partial[3], "gy", 1)
     across = shifted(partial[1] + beyond, "gx", 1)
@@ -358,7 +367,8 @@
 def local(positions, velocities, charges, atom_types, type_radius, tiles, tile_live, destinations):
     clusters = positions.shape[0]
     width = positions.shape[2]
-    mine = lax.axis_index("gy") * lax.axis_size("gx") + lax.axis_index("gx")
+    plate_place = lax.axis_index("gy") * lax.axis_size("gx") + lax.axis_index("gx")
+    mine = jnp.stack([plate_place, 1 - lax.axis_index("gz") % 2])
     tile_count = tiles.shape[0]
     places = jnp.transpose(positions, (1, 0, 2)).reshape(3 * clusters, width)
     moving = jnp.transpose(velocities, (1, 0, 2)).reshape(3 * clusters, width)

time: 79.3 us -> 79.3 us (level)
  starting transfers between devices: 33.4 us -> 32 us
  waiting for transfers between devices: 20.8 us -> 22.2 us
    ppermute x20 -> x12, starting transfers between devices: 26.2 us -> 6.46 us  [shifted(): lax.ppermute(value, axis, [(i, (i + steps) % count) for i in range(count)])]
    ppermute x0 -> x8, starting transfers between devices: none -> 18.4 us  [paired(): return lax.ppermute(value, 'gz', pairs)]
    ppermute x0 -> x8, waiting for transfers between devices: none -> 11.1 us  [paired(): return lax.ppermute(value, 'gz', pairs)]
    ppermute x20 -> x12, waiting for transfers between devices: 13.1 us -> 2.97 us  [shifted(): lax.ppermute(value, axis, [(i, (i + steps) % count) for i in range(count)])]
  transfers between devices with their start and end apart: 22 -> 22, of which waited for: 9 -> 10; matrix products, arithmetic and copies ran while one was open for 4% -> 4% of each run, Pallas kernels for 10% -> 11%
where the time goes in v3:
time: 79.3 us; the launch traced here: 78.9 us
  starting transfers between devices  32 us (40%)
  waiting for transfers between devices  22.2 us (28%)
  Pallas kernels  17.8 us (22%)
  local copies, waits for them, and re-layouts  3.9 us (5%)
  between operations  1.45 us (2%)
  matrix products  0.83 us (1%)
    ppermute x8, starting transfers between devices, paired(): return lax.ppermute(value, 'gz', pairs)  18.4 us
    pallas_call x2, Pallas kernels, tile_forces(): pl.pallas_call(functools.partial(tile_kernel, clusters, tiles), out_shape...  15.1 us
    ppermute x8, waiting for transfers between devices, paired(): return lax.ppermute(value, 'gz', pairs)  11.1 us
    all_to_all x2, waiting for transfers between devices, migrated(): lax.all_to_all(slots, 'gz', split_axis=0, concat_axis=0, tiled=True)  8.2 us
    all_to_all x2, starting transfers between devices, migrated(): lax.all_to_all(slots, 'gz', split_axis=0, concat_axis=0, tiled=True)  7.19 us
    ppermute x12, starting transfers between devices, shifted(): lax.ppermute(value, axis, [(i, (i + steps) % count) for i in range(count)])  6.46 us
    ppermute x12, waiting for transfers between devices, shifted(): lax.ppermute(value, axis, [(i, (i + steps) % count) for i in range(count)])  2.97 us
    unnamed x13, local copies, waits for them, and re-layouts  2.31 us
  transfers between devices with their start and end apart: 22, of which 10 were waited for; matrix products, arithmetic and copies ran while one was open for 4% of the time, Pallas kernels for 11%

profile of v3, /device:TPU:0, one launch (start us, length us, event | category | flops | bytes accessed | tf_op | source)
XLA Modules:
  0.0 78.9 jit_solution(7646921914982687121)
XLA Ops:
  1.3 1.6 %home_array.1.refs_0_.refs_1_.refs_7_ = f32[328,128]{1,0:T(8,128)} custom-call(f32[192,128]{1,0:T(8,128)} %bitcast.58, f32[64,128]{1,0:T(8,128)} %charges.1, s32[64,128]{1,0:T(8,128)} %types.1, f32[16]{0:T(128)} %radii.1, s32[2,256]{1,0:T(2,128)} %bitcast.61, s32[1]{0:T(128)S(6)} %copy.29.live), custom_call_target="tpu_custom_call" | custom-call | tf_op jit(solution)/shard_map/home_array/pallas_call | solution.py:225
  2.9 3.0 %collective-permute-start = (f32[328,128]{1,0:T(8,128)}, f32[328,128]{1,0:T(8,128)S(1)}, u32[]{:S(2)}, u32[]{:S(2)}) collective-permute-start(f32[328,128]{1,0:T(8,128)} %home_array.1.refs_0_.refs_1_.refs_7_), channel_id=1, source_target_pairs={{0,1},{1,0},{2,3},{3,2},{4,5},{5,4},{6,7},{7,6},{8,9},{9,8},{10,11... | collective-permute-start | bytes 503816 | tf_op jit(solution)/shard_map/ppermute | solution.py:26
  5.9 1.5 %collective-permute-start.3 = (f32[328,128]{1,0:T(8,128)}, f32[328,128]{1,0:T(8,128)S(1)}, u32[]{:S(2)}, u32[]{:S(2)}) collective-permute-start(f32[328,128]{1,0:T(8,128)} %home_array.1.refs_0_.refs_1_.refs_7_), channel_id=1, source_target_pairs={{0,4},{4,0},{8,12},{12,8},{16,20},{20,16},{24,28},{28,24},{1,5},{5... | collective-permute-start | bytes 503816 | tf_op jit(solution)/shard_map/ppermute | solution.py:346
  7.4 3.6 %collective-permute-start.4 = (f32[328,128]{1,0:T(8,128)}, f32[328,128]{1,0:T(8,128)S(1)}, u32[]{:S(2)}, u32[]{:S(2)}) collective-permute-start(f32[328,128]{1,0:T(8,128)} %home_array.1.refs_0_.refs_1_.refs_7_), channel_id=1, source_target_pairs={{4,8},{8,4},{12,16},{16,12},{20,24},{24,20},{28,0},{0,28},{5,9},{9... | collective-permute-start | bytes 503816 | tf_op jit(solution)/shard_map/ppermute | solution.py:346
  11.2 1.1 %collective-permute-done.2.refs_3_.refs_4_.refs_10_ = f32[328,128]{1,0:T(8,128)S(1)} collective-permute-done((f32[328,128]{1,0:T(8,128)S(1)}, f32[328,128]{1,0:T(8,128)S(1)}, u32[]{:S(2)}, u32[]{:S(2)}) %collective-permute-start.2) | collective-permute-done | bytes 167968 | tf_op jit(solution)/shard_map/ppermute | solution.py:26
  12.4 0.9 %copy-done = f32[328,128]{1,0:T(8,128)S(1)} copy-done((f32[328,128]{1,0:T(8,128)S(1)}, f32[328,128]{1,0:T(8,128)}, u32[]{:S(2)}) %copy-start) | copy-done | bytes 167960
  13.3 1.1 %plan.1 = s32[8,128]{1,0:T(8,128)S(1)} custom-call(s32[2]{0:T(128)S(1)} %pad_add_fusion.mine, f32[328,128]{1,0:T(8,128)S(1)} %copy-done, f32[328,128]{1,0:T(8,128)S(1)} %collective-permute-done.refs_1_.refs_2_.refs_8_, f32[328,128]{1,0:T(8,128)S(1)} %collective-permute-done.1.refs_2_.refs_3_.refs_9_, ...), custom_call_target="tpu_custom_call" | custom-call | tf_op jit(solution)/shard_map/plan/pallas_call | solution.py:330
  14.4 1.2 %collective-permute-done.3.refs_5_.refs_11_ = f32[328,128]{1,0:T(8,128)S(1)} collective-permute-done((f32[328,128]{1,0:T(8,128)}, f32[328,128]{1,0:T(8,128)S(1)}, u32[]{:S(2)}, u32[]{:S(2)}) %collective-permute-start.3) | collective-permute-done | bytes 167968 | tf_op jit(solution)/shard_map/ppermute | solution.py:346
  15.5 1.2 %collective-permute-done.4.refs_6_.refs_12_ = f32[328,128]{1,0:T(8,128)S(1)} collective-permute-done((f32[328,128]{1,0:T(8,128)}, f32[328,128]{1,0:T(8,128)S(1)}, u32[]{:S(2)}, u32[]{:S(2)}) %collective-permute-start.4) | collective-permute-done | bytes 167968 | tf_op jit(solution)/shard_map/ppermute | solution.py:346
  16.7 7.6 %tile_forces.2 = (f32[192,128]{1,0:T(8,128)S(1)}, f32[192,128]{1,0:T(8,128)S(1)}, f32[192,128]{1,0:T(8,128)S(1)}, f32[192,128]{1,0:T(8,128)S(1)}, f32[192,128]{1,0:T(8,128)S(1)}, /*index=5*/f32[192,128]{1,0:T(8,128)S(1)}) custom-call(s32[1024]{0:T(1024)S(1)} %bitcast.49, f32[328,128]{1,0:T(8,128)S(1)} %copy-done.1, ...), custom_call_target="tpu_custom_call" | custom-call | flops 8589934592 | bytes 4194304 | tf_op jit(solution)/shard_map/tile_forces/pallas_call | solution.py:185
  24.6 5.4 %collective-permute-start.9 = (f32[192,128]{1,0:T(8,128)S(1)}, f32[192,128]{1,0:T(8,128)S(1)}, u32[]{:S(2)}, u32[]{:S(2)}) collective-permute-start(f32[192,128]{1,0:T(8,128)S(1)} %get-tuple-element.19), channel_id=1, source_target_pairs={{4,8},{8,4},{12,16},{16,12},{20,24},{24,20},{28,0},{0,28},{5,9},{9... | collective-permute-start | bytes 294920 | tf_op jit(solution)/shard_map/ppermute | solution.py:346
  30.2 0.6 collective-permute-start.7
  30.8 2.7 %collective-permute-done.9 = f32[192,128]{1,0:T(8,128)S(1)} collective-permute-done((f32[192,128]{1,0:T(8,128)S(1)}, f32[192,128]{1,0:T(8,128)S(1)}, u32[]{:S(2)}, u32[]{:S(2)}) %collective-permute-start.9) | collective-permute-done | bytes 98336 | tf_op jit(solution)/shard_map/ppermute | solution.py:346
  33.5 2.0 %collective-permute-done.8 = f32[192,128]{1,0:T(8,128)S(1)} collective-permute-done((f32[192,128]{1,0:T(8,128)S(1)}, f32[192,128]{1,0:T(8,128)S(1)}, u32[]{:S(2)}, u32[]{:S(2)}) %collective-permute-start.8) | collective-permute-done | bytes 98336 | tf_op jit(solution)/shard_map/ppermute | solution.py:346
  35.6 0.6 collective-permute-start.10
  36.2 1.8 %collective-permute-start.13 = (f32[192,128]{1,0:T(8,128)S(1)}, f32[192,128]{1,0:T(8,128)S(1)}, u32[]{:S(2)}, u32[]{:S(2)}) collective-permute-start(f32[192,128]{1,0:T(8,128)S(1)} %get-tuple-element.28.refs_1_), channel_id=1, source_target_pairs={{0,4},{4,0},{8,12},{12,8},{16,20},{20,16},{24,28},{28,24},{1,5},{5... | collective-permute-start | bytes 294920 | tf_op jit(solution)/shard_map/ppermute | solution.py:346
  37.9 0.6 collective-permute-start.14
  38.6 1.8 %collective-permute-done.10.refs_2_ = f32[192,128]{1,0:T(8,128)S(1)} collective-permute-done((f32[192,128]{1,0:T(8,128)S(1)}, f32[192,128]{1,0:T(8,128)S(1)}, u32[]{:S(2)}, u32[]{:S(2)}) %collective-permute-start.10) | collective-permute-done | bytes 98336 | tf_op jit(solution)/shard_map/ppermute | solution.py:26
  40.4 0.5 fusion.4
  40.8 0.8 %copy.27 = f32[8,8,16,128]{3,2,0,1:T(8,128)} copy(f32[8,8,16,128]{3,2,1,0:T(8,128)S(1)} %bitcast.53) | data formatting | bytes 1048576 | tf_op jit(solution)/shard_map/reshape | solution.py:390
  41.7 3.7 %all-to-all-start = ((f32[8,8,16,128]{3,2,1,0:T(8,128)}), f32[8,8,16,128]{3,2,1,0:T(8,128)S(1)}, u32[]{:S(2)}, u32[]{:S(2)}) async-start(f32[8,8,16,128]{3,2,1,0:T(8,128)} %bitcast.47), calls=%async_computation | async-start | bytes 1048576 | tf_op jit(solution)/shard_map/all_to_all | solution.py:391
  45.6 7.6 %tile_forces.3 = (f32[192,128]{1,0:T(8,128)S(1)}, f32[192,128]{1,0:T(8,128)S(1)}, f32[192,128]{1,0:T(8,128)S(1)}, f32[192,128]{1,0:T(8,128)S(1)}, f32[192,128]{1,0:T(8,128)S(1)}, /*index=5*/f32[192,128]{1,0:T(8,128)S(1)}) custom-call(s32[1024]{0:T(1024)S(1)} %bitcast.50, f32[192,128]{1,0:T(8,128)S(1)} %get-tuple-element.28.refs_1_, ...), custom_call_target="tpu_custom_call" | custom-call | flops 8589934592 | bytes 4194304 | tf_op jit(solution)/shard_map/tile_forces/pallas_call | solution.py:185
  53.1 0.3 collective-permute-start.16
  53.4 5.6 %collective-permute-start.19 = (f32[192,128]{1,0:T(8,128)S(1)}, f32[192,128]{1,0:T(8,128)S(1)}, u32[]{:S(2)}, u32[]{:S(2)}) collective-permute-start(f32[192,128]{1,0:T(8,128)S(1)} %get-tuple-element.25), channel_id=1, source_target_pairs={{4,8},{8,4},{12,16},{16,12},{20,24},{24,20},{28,0},{0,28},{5,9},{9... | collective-permute-start | bytes 294920 | tf_op jit(solution)/shard_map/ppermute | solution.py:346
  59.1 1.6 %collective-permute-start.17 = (f32[192,128]{1,0:T(8,128)S(1)}, f32[192,128]{1,0:T(8,128)S(1)}, u32[]{:S(2)}, u32[]{:S(2)}) collective-permute-start(f32[192,128]{1,0:T(8,128)S(1)} %add.69), channel_id=1, source_target_pairs={{0,1},{1,0},{2,3},{3,2},{4,5},{5,4},{6,7},{7,6},{8,9},{9,8},{10,11... | collective-permute-start | bytes 294920 | tf_op jit(solution)/shard_map/ppermute | solution.py:26
  60.7 1.8 %collective-permute-done.19 = f32[192,128]{1,0:T(8,128)S(1)} collective-permute-done((f32[192,128]{1,0:T(8,128)S(1)}, f32[192,128]{1,0:T(8,128)S(1)}, u32[]{:S(2)}, u32[]{:S(2)}) %collective-permute-start.19) | collective-permute-done | bytes 98336 | tf_op jit(solution)/shard_map/ppermute | solution.py:346
  62.5 2.0 %collective-permute-done.18 = f32[192,128]{1,0:T(8,128)S(1)} collective-permute-done((f32[192,128]{1,0:T(8,128)S(1)}, f32[192,128]{1,0:T(8,128)S(1)}, u32[]{:S(2)}, u32[]{:S(2)}) %collective-permute-start.18) | collective-permute-done | bytes 98336 | tf_op jit(solution)/shard_map/ppermute | solution.py:346
  64.6 0.4 fusion.2
  65.2 0.7 copy.28
  66.0 3.5 %all-to-all-start.1 = ((f32[8,3,16,128]{3,2,1,0:T(8,128)}), f32[8,3,16,128]{3,2,1,0:T(8,128)S(1)}, u32[]{:S(2)}, u32[]{:S(2)}) async-start(f32[8,3,16,128]{3,2,1,0:T(8,128)} %bitcast.48), calls=%async_computation.1 | async-start | bytes 393216 | tf_op jit(solution)/shard_map/all_to_all | solution.py:391
  69.5 8.2 %all-to-all-done.1 = f32[8,3,16,128]{3,2,1,0:T(8,128)S(1)} async-done(((f32[8,3,16,128]{3,2,1,0:T(8,128)}), f32[8,3,16,128]{3,2,1,0:T(8,128)S(1)}, u32[]{:S(2)}, u32[]{:S(2)}) %all-to-all-start.1) | async-done | bytes 196640 | tf_op jit(solution)/shard_map/all_to_all | solution.py:391
  77.8 1.1 %copy.19 = f32[128,8,128]{2,1,0:T(8,128)} copy(f32[128,8,128]{2,0,1:T(8,128)S(1)} %maximum_bitcast_fusion) | data formatting | bytes 1048576
  (49 shorter events, 1.7 us)
Async XLA Ops:
  2.9 8.1 %copy-start.5 = (s32[64,1]{0,1:T(1,128)S(1)}, s32[64,1]{0,1:T(1,128)}, u32[]{:S(2)}) copy-start(s32[64,1]{0,1:T(1,128)} %param.15) | copy-start | bytes 772
  2.9 8.1 %collective-permute-start = (f32[328,128]{1,0:T(8,128)}, f32[328,128]{1,0:T(8,128)S(1)}, u32[]{:S(2)}, u32[]{:S(2)}) collective-permute-start(f32[328,128]{1,0:T(8,128)} %home_array.1.refs_0_.refs_1_.refs_7_), channel_id=1, source_target_pairs={{0,1},{1,0},{2,3},{3,2},{4,5},{5,4},{6,7},{7,6},{8,9},{9,8},{10,11... | collective-permute-start | bytes 503816 | tf_op jit(solution)/shard_map/ppermute | solution.py:26
  5.9 5.3 %collective-permute-start.1 = (f32[328,128]{1,0:T(8,128)}, f32[328,128]{1,0:T(8,128)S(1)}, u32[]{:S(2)}, u32[]{:S(2)}) collective-permute-start(f32[328,128]{1,0:T(8,128)} %home_array.1.refs_0_.refs_1_.refs_7_), channel_id=1, source_target_pairs={{0,2},{2,0},{1,3},{3,1},{4,6},{6,4},{5,7},{7,5},{8,10},{10,8},{9,1... | collective-permute-start | bytes 503816 | tf_op jit(solution)/shard_map/ppermute | solution.py:26
  5.9 9.6 %collective-permute-start.3 = (f32[328,128]{1,0:T(8,128)}, f32[328,128]{1,0:T(8,128)S(1)}, u32[]{:S(2)}, u32[]{:S(2)}) collective-permute-start(f32[328,128]{1,0:T(8,128)} %home_array.1.refs_0_.refs_1_.refs_7_), channel_id=1, source_target_pairs={{0,4},{4,0},{8,12},{12,8},{16,20},{20,16},{24,28},{28,24},{1,5},{5... | collective-permute-start | bytes 503816 | tf_op jit(solution)/shard_map/ppermute | solution.py:346
  7.4 9.3 %collective-permute-start.4 = (f32[328,128]{1,0:T(8,128)}, f32[328,128]{1,0:T(8,128)S(1)}, u32[]{:S(2)}, u32[]{:S(2)}) collective-permute-start(f32[328,128]{1,0:T(8,128)} %home_array.1.refs_0_.refs_1_.refs_7_), channel_id=1, source_target_pairs={{4,8},{8,4},{12,16},{16,12},{20,24},{24,20},{28,0},{0,28},{5,9},{9... | collective-permute-start | bytes 503816 | tf_op jit(solution)/shard_map/ppermute | solution.py:346
  11.0 1.4 %collective-permute-start.2 = (f32[328,128]{1,0:T(8,128)S(1)}, f32[328,128]{1,0:T(8,128)S(1)}, u32[]{:S(2)}, u32[]{:S(2)}) collective-permute-start(f32[328,128]{1,0:T(8,128)S(1)} %collective-permute-done.refs_1_.refs_2_.refs_8_), channel_id=1, source_target_pairs={{0,2},{2,0},{1,3},{3,1},{4,6},{6,4},{5,7},{7,5},{8,10},{10,8},{9,1... | collective-permute-start | bytes 503816 | tf_op jit(solution)/shard_map/ppermute | solution.py:26
  12.4 0.9 %copy-start = (f32[328,128]{1,0:T(8,128)S(1)}, f32[328,128]{1,0:T(8,128)}, u32[]{:S(2)}) copy-start(f32[328,128]{1,0:T(8,128)} %home_array.1.refs_0_.refs_1_.refs_7_) | copy-start | bytes 503812
  13.3 3.4 %copy-start.1 = (f32[328,128]{1,0:T(8,128)S(1)}, f32[328,128]{1,0:T(8,128)}, u32[]{:S(2)}) copy-start(f32[328,128]{1,0:T(8,128)} %home_array.1.refs_0_.refs_1_.refs_7_) | copy-start | bytes 503812
  24.3 5.9 %collective-permute-start.6 = (f32[192,128]{1,0:T(8,128)S(1)}, f32[192,128]{1,0:T(8,128)S(1)}, u32[]{:S(2)}, u32[]{:S(2)}) collective-permute-start(f32[192,128]{1,0:T(8,128)S(1)} %get-tuple-element.17), channel_id=1, source_target_pairs={{0,2},{2,0},{1,3},{3,1},{4,6},{6,4},{5,7},{7,5},{8,10},{10,8},{9,1... | collective-permute-start | bytes 294920 | tf_op jit(solution)/shard_map/ppermute | solution.py:26
  24.6 8.9 %collective-permute-start.9 = (f32[192,128]{1,0:T(8,128)S(1)}, f32[192,128]{1,0:T(8,128)S(1)}, u32[]{:S(2)}, u32[]{:S(2)}) collective-permute-start(f32[192,128]{1,0:T(8,128)S(1)} %get-tuple-element.19), channel_id=1, source_target_pairs={{4,8},{8,4},{12,16},{16,12},{20,24},{24,20},{28,0},{0,28},{5,9},{9... | collective-permute-start | bytes 294920 | tf_op jit(solution)/shard_map/ppermute | solution.py:346
  30.0 5.6 %collective-permute-start.8 = (f32[192,128]{1,0:T(8,128)S(1)}, f32[192,128]{1,0:T(8,128)S(1)}, u32[]{:S(2)}, u32[]{:S(2)}) collective-permute-start(f32[192,128]{1,0:T(8,128)S(1)} %get-tuple-element.18), channel_id=1, source_target_pairs={{0,4},{4,0},{8,12},{12,8},{16,20},{20,16},{24,28},{28,24},{1,5},{5... | collective-permute-start | bytes 294920 | tf_op jit(solution)/shard_map/ppermute | solution.py:346
  30.0 5.6 %collective-permute-start.5 = (f32[192,128]{1,0:T(8,128)S(1)}, f32[192,128]{1,0:T(8,128)S(1)}, u32[]{:S(2)}, u32[]{:S(2)}) collective-permute-start(f32[192,128]{1,0:T(8,128)S(1)} %get-tuple-element.15), channel_id=1, source_target_pairs={{0,2},{2,0},{1,3},{3,1},{4,6},{6,4},{5,7},{7,5},{8,10},{10,8},{9,1... | collective-permute-start | bytes 294920 | tf_op jit(solution)/shard_map/ppermute | solution.py:26
  30.2 5.3 %copy-start.4 = (f32[64,3,128]{2,0,1:T(8,128)S(1)}, f32[64,3,128]{2,0,1:T(8,128)}, u32[]{:S(2)}) copy-start(f32[64,3,128]{2,0,1:T(8,128)} %param.9) | copy-start | bytes 294916
  30.2 5.3 %copy-start.2 = (f32[64,3,128]{2,0,1:T(8,128)S(1)}, f32[64,3,128]{2,0,1:T(8,128)}, u32[]{:S(2)}) copy-start(f32[64,3,128]{2,0,1:T(8,128)} %param.8) | copy-start | bytes 294916
  30.2 5.3 %collective-permute-start.7 = (f32[192,128]{1,0:T(8,128)S(1)}, f32[192,128]{1,0:T(8,128)S(1)}, u32[]{:S(2)}, u32[]{:S(2)}) collective-permute-start(f32[192,128]{1,0:T(8,128)S(1)} %add.62), channel_id=1, source_target_pairs={{0,1},{1,0},{2,3},{3,2},{4,5},{5,4},{6,7},{7,6},{8,9},{9,8},{10,11... | collective-permute-start | bytes 294920 | tf_op jit(solution)/shard_map/ppermute | solution.py:26
  35.6 4.8 %collective-permute-start.10 = (f32[192,128]{1,0:T(8,128)S(1)}, f32[192,128]{1,0:T(8,128)S(1)}, u32[]{:S(2)}, u32[]{:S(2)}) collective-permute-start(f32[192,128]{1,0:T(8,128)S(1)} %get-tuple-element.28.refs_1_), channel_id=1, source_target_pairs={{0,1},{1,0},{2,3},{3,2},{4,5},{5,4},{6,7},{7,6},{8,9},{9,8},{10,11... | collective-permute-start | bytes 294920 | tf_op jit(solution)/shard_map/ppermute | solution.py:26
  36.2 9.2 %collective-permute-start.11 = (f32[192,128]{1,0:T(8,128)S(1)}, f32[192,128]{1,0:T(8,128)S(1)}, u32[]{:S(2)}, u32[]{:S(2)}) collective-permute-start(f32[192,128]{1,0:T(8,128)S(1)} %get-tuple-element.28.refs_1_), channel_id=1, source_target_pairs={{0,2},{2,0},{1,3},{3,1},{4,6},{6,4},{5,7},{7,5},{8,10},{10,8},{9,1... | collective-permute-start | bytes 294920 | tf_op jit(solution)/shard_map/ppermute | solution.py:26
  36.2 9.2 %collective-permute-start.13 = (f32[192,128]{1,0:T(8,128)S(1)}, f32[192,128]{1,0:T(8,128)S(1)}, u32[]{:S(2)}, u32[]{:S(2)}) collective-permute-start(f32[192,128]{1,0:T(8,128)S(1)} %get-tuple-element.28.refs_1_), channel_id=1, source_target_pairs={{0,4},{4,0},{8,12},{12,8},{16,20},{20,16},{24,28},{28,24},{1,5},{5... | collective-permute-start | bytes 294920 | tf_op jit(solution)/shard_map/ppermute | solution.py:346
  37.9 7.6 %collective-permute-start.14 = (f32[192,128]{1,0:T(8,128)S(1)}, f32[192,128]{1,0:T(8,128)S(1)}, u32[]{:S(2)}, u32[]{:S(2)}) collective-permute-start(f32[192,128]{1,0:T(8,128)S(1)} %get-tuple-element.28.refs_1_), channel_id=1, source_target_pairs={{4,8},{8,4},{12,16},{16,12},{20,24},{24,20},{28,0},{0,28},{5,9},{9... | collective-permute-start | bytes 294920 | tf_op jit(solution)/shard_map/ppermute | solution.py:346
  40.4 5.2 %collective-permute-start.12 = (f32[192,128]{1,0:T(8,128)S(1)}, f32[192,128]{1,0:T(8,128)S(1)}, u32[]{:S(2)}, u32[]{:S(2)}) collective-permute-start(f32[192,128]{1,0:T(8,128)S(1)} %collective-permute-done.10.refs_2_), channel_id=1, source_target_pairs={{0,2},{2,0},{1,3},{3,1},{4,6},{6,4},{5,7},{7,5},{8,10},{10,8},{9,1... | collective-permute-start | bytes 294920 | tf_op jit(solution)/shard_map/ppermute | solution.py:26
  41.7 24.3 %all-to-all-start = ((f32[8,8,16,128]{3,2,1,0:T(8,128)}), f32[8,8,16,128]{3,2,1,0:T(8,128)S(1)}, u32[]{:S(2)}, u32[]{:S(2)}) async-start(f32[8,8,16,128]{3,2,1,0:T(8,128)} %bitcast.47), calls=%async_computation | async-start | bytes 1048576 | tf_op jit(solution)/shard_map/all_to_all | solution.py:391
  53.1 6.0 %collective-permute-start.16 = (f32[192,128]{1,0:T(8,128)S(1)}, f32[192,128]{1,0:T(8,128)S(1)}, u32[]{:S(2)}, u32[]{:S(2)}) collective-permute-start(f32[192,128]{1,0:T(8,128)S(1)} %get-tuple-element.23), channel_id=1, source_target_pairs={{0,2},{2,0},{1,3},{3,1},{4,6},{6,4},{5,7},{7,5},{8,10},{10,8},{9,1... | collective-permute-start | bytes 294920 | tf_op jit(solution)/shard_map/ppermute | solution.py:26
  53.4 9.1 %collective-permute-start.19 = (f32[192,128]{1,0:T(8,128)S(1)}, f32[192,128]{1,0:T(8,128)S(1)}, u32[]{:S(2)}, u32[]{:S(2)}) collective-permute-start(f32[192,128]{1,0:T(8,128)S(1)} %get-tuple-element.25), channel_id=1, source_target_pairs={{4,8},{8,4},{12,16},{16,12},{20,24},{24,20},{28,0},{0,28},{5,9},{9... | collective-permute-start | bytes 294920 | tf_op jit(solution)/shard_map/ppermute | solution.py:346
  59.0 5.6 %collective-permute-start.18 = (f32[192,128]{1,0:T(8,128)S(1)}, f32[192,128]{1,0:T(8,128)S(1)}, u32[]{:S(2)}, u32[]{:S(2)}) collective-permute-start(f32[192,128]{1,0:T(8,128)S(1)} %get-tuple-element.24), channel_id=1, source_target_pairs={{0,4},{4,0},{8,12},{12,8},{16,20},{20,16},{24,28},{28,24},{1,5},{5... | collective-permute-start | bytes 294920 | tf_op jit(solution)/shard_map/ppermute | solution.py:346
  59.0 5.6 %collective-permute-start.15 = (f32[192,128]{1,0:T(8,128)S(1)}, f32[192,128]{1,0:T(8,128)S(1)}, u32[]{:S(2)}, u32[]{:S(2)}) collective-permute-start(f32[192,128]{1,0:T(8,128)S(1)} %get-tuple-element.21), channel_id=1, source_target_pairs={{0,2},{2,0},{1,3},{3,1},{4,6},{6,4},{5,7},{7,5},{8,10},{10,8},{9,1... | collective-permute-start | bytes 294920 | tf_op jit(solution)/shard_map/ppermute | solution.py:26
  59.1 5.4 %collective-permute-start.17 = (f32[192,128]{1,0:T(8,128)S(1)}, f32[192,128]{1,0:T(8,128)S(1)}, u32[]{:S(2)}, u32[]{:S(2)}) collective-permute-start(f32[192,128]{1,0:T(8,128)S(1)} %add.69), channel_id=1, source_target_pairs={{0,1},{1,0},{2,3},{3,2},{4,5},{5,4},{6,7},{7,6},{8,9},{9,8},{10,11... | collective-permute-start | bytes 294920 | tf_op jit(solution)/shard_map/ppermute | solution.py:26
  64.6 0.6 copy-start.3
  66.0 11.8 %all-to-all-start.1 = ((f32[8,3,16,128]{3,2,1,0:T(8,128)}), f32[8,3,16,128]{3,2,1,0:T(8,128)S(1)}, u32[]{:S(2)}, u32[]{:S(2)}) async-start(f32[8,3,16,128]{3,2,1,0:T(8,128)} %bitcast.48), calls=%async_computation.1 | async-start | bytes 393216 | tf_op jit(solution)/shard_map/all_to_all | solution.py:391

commit v4 on v3

--- a/solution.py
+++ b/solution.py
@@ -161,7 +161,16 @@
 
     phase(0, even, odd, filling=2)
     phase(1, odd, even, filling=1)
-    lax.fori_loop(1, 1 + (live + 2 * half - 1) // (2 * half), group, 0)
+    groups = (live + half - 1) // half
+    lax.fori_loop(1, 1 + groups // 2, group, 0)
+
+    @pl.when(groups % 2 == 1)
+    def _():
+        final = [pushes((groups - 1) * half + u, even[1:], u) for u in range(half)]
+        for left_at, right_at, on_left, on_right in final:
+            totals[pl.ds(left_at, 8), :] += on_left
+            totals[pl.ds(right_at, 8), :] += on_right
+
     for piece in range(6):
         first = piece * clusters * moment_rows
 

time: 79.3 us -> 77.8 us (0.981)
  Pallas kernels: 17.8 us -> 16.4 us
  waiting for transfers between devices: 22.2 us -> 21.3 us
  starting transfers between devices: 32 us -> 32.8 us
    pallas_call x2, Pallas kernels: 15.1 us -> 13.7 us  [tile_forces(): pl.pallas_call(functools.partial(tile_kernel, clusters, tiles), out_shape...]
  transfers between devices with their start and end apart: 22 -> 22, of which waited for: 10 -> 10; matrix products, arithmetic and copies ran while one was open for 4% -> 4% of each run, Pallas kernels for 11% -> 10%
where the time goes in v4:
time: 77.8 us; the launch traced here: 77.4 us
  starting transfers between devices  32.8 us (42%)
  waiting for transfers between devices  21.3 us (27%)
  Pallas kernels  16.4 us (21%)
  local copies, waits for them, and re-layouts  3.9 us (5%)
  between operations  1.44 us (2%)
  matrix products  0.84 us (1%)
    ppermute x8, starting transfers between devices, paired(): return lax.ppermute(value, 'gz', pairs)  19.1 us
    pallas_call x2, Pallas kernels, tile_forces(): pl.pallas_call(functools.partial(tile_kernel, clusters, tiles), out_shape...  13.7 us
    ppermute x8, waiting for transfers between devices, paired(): return lax.ppermute(value, 'gz', pairs)  11 us
    all_to_all x2, waiting for transfers between devices, migrated(): lax.all_to_all(slots, 'gz', split_axis=0, concat_axis=0, tiled=True)  8.06 us
    all_to_all x2, starting transfers between devices, migrated(): lax.all_to_all(slots, 'gz', split_axis=0, concat_axis=0, tiled=True)  7.25 us
    ppermute x12, starting transfers between devices, shifted(): lax.ppermute(value, axis, [(i, (i + steps) % count) for i in range(count)])  6.48 us
    unnamed x13, local copies, waits for them, and re-layouts  2.31 us
    ppermute x12, waiting for transfers between devices, shifted(): lax.ppermute(value, axis, [(i, (i + steps) % count) for i in range(count)])  2.26 us
  transfers between devices with their start and end apart: 22, of which 10 were waited for; matrix products, arithmetic and copies ran while one was open for 4% of the time, Pallas kernels for 10%

profile of v4, /device:TPU:0, one launch (start us, length us, event | category | flops | bytes accessed | tf_op | source)
XLA Modules:
  0.0 77.4 jit_solution(18197375425888131782)
XLA Ops:
  1.3 1.6 %home_array.1.refs_0_.refs_1_.refs_7_ = f32[328,128]{1,0:T(8,128)} custom-call(f32[192,128]{1,0:T(8,128)} %bitcast.58, f32[64,128]{1,0:T(8,128)} %charges.1, s32[64,128]{1,0:T(8,128)} %types.1, f32[16]{0:T(128)} %radii.1, s32[2,256]{1,0:T(2,128)} %bitcast.61, s32[1]{0:T(128)S(6)} %copy.29.live), custom_call_target="tpu_custom_call" | custom-call | tf_op jit(solution)/shard_map/home_array/pallas_call | solution.py:234
  2.9 3.0 %collective-permute-start = (f32[328,128]{1,0:T(8,128)}, f32[328,128]{1,0:T(8,128)S(1)}, u32[]{:S(2)}, u32[]{:S(2)}) collective-permute-start(f32[328,128]{1,0:T(8,128)} %home_array.1.refs_0_.refs_1_.refs_7_), channel_id=1, source_target_pairs={{0,1},{1,0},{2,3},{3,2},{4,5},{5,4},{6,7},{7,6},{8,9},{9,8},{10,11... | collective-permute-start | bytes 503816 | tf_op jit(solution)/shard_map/ppermute | solution.py:26
  5.9 1.5 %collective-permute-start.3 = (f32[328,128]{1,0:T(8,128)}, f32[328,128]{1,0:T(8,128)S(1)}, u32[]{:S(2)}, u32[]{:S(2)}) collective-permute-start(f32[328,128]{1,0:T(8,128)} %home_array.1.refs_0_.refs_1_.refs_7_), channel_id=1, source_target_pairs={{0,4},{4,0},{8,12},{12,8},{16,20},{20,16},{24,28},{28,24},{1,5},{5... | collective-permute-start | bytes 503816 | tf_op jit(solution)/shard_map/ppermute | solution.py:355
  7.4 3.6 %collective-permute-start.4 = (f32[328,128]{1,0:T(8,128)}, f32[328,128]{1,0:T(8,128)S(1)}, u32[]{:S(2)}, u32[]{:S(2)}) collective-permute-start(f32[328,128]{1,0:T(8,128)} %home_array.1.refs_0_.refs_1_.refs_7_), channel_id=1, source_target_pairs={{4,8},{8,4},{12,16},{16,12},{20,24},{24,20},{28,0},{0,28},{5,9},{9... | collective-permute-start | bytes 503816 | tf_op jit(solution)/shard_map/ppermute | solution.py:355
  11.2 1.1 %collective-permute-done.2.refs_3_.refs_4_.refs_10_ = f32[328,128]{1,0:T(8,128)S(1)} collective-permute-done((f32[328,128]{1,0:T(8,128)S(1)}, f32[328,128]{1,0:T(8,128)S(1)}, u32[]{:S(2)}, u32[]{:S(2)}) %collective-permute-start.2) | collective-permute-done | bytes 167968 | tf_op jit(solution)/shard_map/ppermute | solution.py:26
  12.4 0.9 %copy-done = f32[328,128]{1,0:T(8,128)S(1)} copy-done((f32[328,128]{1,0:T(8,128)S(1)}, f32[328,128]{1,0:T(8,128)}, u32[]{:S(2)}) %copy-start) | copy-done | bytes 167960
  13.3 1.1 %plan.1 = s32[8,128]{1,0:T(8,128)S(1)} custom-call(s32[2]{0:T(128)S(1)} %pad_add_fusion.mine, f32[328,128]{1,0:T(8,128)S(1)} %copy-done, f32[328,128]{1,0:T(8,128)S(1)} %collective-permute-done.refs_1_.refs_2_.refs_8_, f32[328,128]{1,0:T(8,128)S(1)} %collective-permute-done.1.refs_2_.refs_3_.refs_9_, ...), custom_call_target="tpu_custom_call" | custom-call | tf_op jit(solution)/shard_map/plan/pallas_call | solution.py:339
  14.4 1.2 %collective-permute-done.3.refs_5_.refs_11_ = f32[328,128]{1,0:T(8,128)S(1)} collective-permute-done((f32[328,128]{1,0:T(8,128)}, f32[328,128]{1,0:T(8,128)S(1)}, u32[]{:S(2)}, u32[]{:S(2)}) %collective-permute-start.3) | collective-permute-done | bytes 167968 | tf_op jit(solution)/shard_map/ppermute | solution.py:355
  15.5 1.2 %collective-permute-done.4.refs_6_.refs_12_ = f32[328,128]{1,0:T(8,128)S(1)} collective-permute-done((f32[328,128]{1,0:T(8,128)}, f32[328,128]{1,0:T(8,128)S(1)}, u32[]{:S(2)}, u32[]{:S(2)}) %collective-permute-start.4) | collective-permute-done | bytes 167968 | tf_op jit(solution)/shard_map/ppermute | solution.py:355
  16.7 6.9 %tile_forces.2 = (f32[192,128]{1,0:T(8,128)S(1)}, f32[192,128]{1,0:T(8,128)S(1)}, f32[192,128]{1,0:T(8,128)S(1)}, f32[192,128]{1,0:T(8,128)S(1)}, f32[192,128]{1,0:T(8,128)S(1)}, /*index=5*/f32[192,128]{1,0:T(8,128)S(1)}) custom-call(s32[1024]{0:T(1024)S(1)} %bitcast.49, f32[328,128]{1,0:T(8,128)S(1)} %copy-done.1, ...), custom_call_target="tpu_custom_call" | custom-call | flops 8589934592 | bytes 4194304 | tf_op jit(solution)/shard_map/tile_forces/pallas_call | solution.py:194
  23.9 5.4 %collective-permute-start.9 = (f32[192,128]{1,0:T(8,128)S(1)}, f32[192,128]{1,0:T(8,128)S(1)}, u32[]{:S(2)}, u32[]{:S(2)}) collective-permute-start(f32[192,128]{1,0:T(8,128)S(1)} %get-tuple-element.19), channel_id=1, source_target_pairs={{4,8},{8,4},{12,16},{16,12},{20,24},{24,20},{28,0},{0,28},{5,9},{9... | collective-permute-start | bytes 294920 | tf_op jit(solution)/shard_map/ppermute | solution.py:355
  29.5 0.6 collective-permute-start.7
  30.1 2.7 %collective-permute-done.9 = f32[192,128]{1,0:T(8,128)S(1)} collective-permute-done((f32[192,128]{1,0:T(8,128)S(1)}, f32[192,128]{1,0:T(8,128)S(1)}, u32[]{:S(2)}, u32[]{:S(2)}) %collective-permute-start.9) | collective-permute-done | bytes 98336 | tf_op jit(solution)/shard_map/ppermute | solution.py:355
  32.8 2.0 %collective-permute-done.8 = f32[192,128]{1,0:T(8,128)S(1)} collective-permute-done((f32[192,128]{1,0:T(8,128)S(1)}, f32[192,128]{1,0:T(8,128)S(1)}, u32[]{:S(2)}, u32[]{:S(2)}) %collective-permute-start.8) | collective-permute-done | bytes 98336 | tf_op jit(solution)/shard_map/ppermute | solution.py:355
  34.9 0.6 collective-permute-start.10
  35.5 1.8 %collective-permute-start.13 = (f32[192,128]{1,0:T(8,128)S(1)}, f32[192,128]{1,0:T(8,128)S(1)}, u32[]{:S(2)}, u32[]{:S(2)}) collective-permute-start(f32[192,128]{1,0:T(8,128)S(1)} %get-tuple-element.28.refs_1_), channel_id=1, source_target_pairs={{0,4},{4,0},{8,12},{12,8},{16,20},{20,16},{24,28},{28,24},{1,5},{5... | collective-permute-start | bytes 294920 | tf_op jit(solution)/shard_map/ppermute | solution.py:355
  37.2 1.3 %collective-permute-start.14 = (f32[192,128]{1,0:T(8,128)S(1)}, f32[192,128]{1,0:T(8,128)S(1)}, u32[]{:S(2)}, u32[]{:S(2)}) collective-permute-start(f32[192,128]{1,0:T(8,128)S(1)} %get-tuple-element.28.refs_1_), channel_id=1, source_target_pairs={{4,8},{8,4},{12,16},{16,12},{20,24},{24,20},{28,0},{0,28},{5,9},{9... | collective-permute-start | bytes 294920 | tf_op jit(solution)/shard_map/ppermute | solution.py:355
  38.6 1.1 %collective-permute-done.10.refs_2_ = f32[192,128]{1,0:T(8,128)S(1)} collective-permute-done((f32[192,128]{1,0:T(8,128)S(1)}, f32[192,128]{1,0:T(8,128)S(1)}, u32[]{:S(2)}, u32[]{:S(2)}) %collective-permute-start.10) | collective-permute-done | bytes 98336 | tf_op jit(solution)/shard_map/ppermute | solution.py:26
  39.7 0.5 fusion.4
  40.1 0.8 %copy.27 = f32[8,8,16,128]{3,2,0,1:T(8,128)} copy(f32[8,8,16,128]{3,2,1,0:T(8,128)S(1)} %bitcast.53) | data formatting | bytes 1048576 | tf_op jit(solution)/shard_map/reshape | solution.py:399
  41.0 3.7 %all-to-all-start = ((f32[8,8,16,128]{3,2,1,0:T(8,128)}), f32[8,8,16,128]{3,2,1,0:T(8,128)S(1)}, u32[]{:S(2)}, u32[]{:S(2)}) async-start(f32[8,8,16,128]{3,2,1,0:T(8,128)} %bitcast.47), calls=%async_computation | async-start | bytes 1048576 | tf_op jit(solution)/shard_map/all_to_all | solution.py:400
  44.8 6.9 %tile_forces.3 = (f32[192,128]{1,0:T(8,128)S(1)}, f32[192,128]{1,0:T(8,128)S(1)}, f32[192,128]{1,0:T(8,128)S(1)}, f32[192,128]{1,0:T(8,128)S(1)}, f32[192,128]{1,0:T(8,128)S(1)}, /*index=5*/f32[192,128]{1,0:T(8,128)S(1)}) custom-call(s32[1024]{0:T(1024)S(1)} %bitcast.50, f32[192,128]{1,0:T(8,128)S(1)} %get-tuple-element.28.refs_1_, ...), custom_call_target="tpu_custom_call" | custom-call | flops 8589934592 | bytes 4194304 | tf_op jit(solution)/shard_map/tile_forces/pallas_call | solution.py:194
  51.7 0.3 collective-permute-start.16
  52.0 5.5 %collective-permute-start.19 = (f32[192,128]{1,0:T(8,128)S(1)}, f32[192,128]{1,0:T(8,128)S(1)}, u32[]{:S(2)}, u32[]{:S(2)}) collective-permute-start(f32[192,128]{1,0:T(8,128)S(1)} %get-tuple-element.25), channel_id=1, source_target_pairs={{4,8},{8,4},{12,16},{16,12},{20,24},{24,20},{28,0},{0,28},{5,9},{9... | collective-permute-start | bytes 294920 | tf_op jit(solution)/shard_map/ppermute | solution.py:355
  57.7 1.6 %collective-permute-start.17 = (f32[192,128]{1,0:T(8,128)S(1)}, f32[192,128]{1,0:T(8,128)S(1)}, u32[]{:S(2)}, u32[]{:S(2)}) collective-permute-start(f32[192,128]{1,0:T(8,128)S(1)} %add.69), channel_id=1, source_target_pairs={{0,1},{1,0},{2,3},{3,2},{4,5},{5,4},{6,7},{7,6},{8,9},{9,8},{10,11... | collective-permute-start | bytes 294920 | tf_op jit(solution)/shard_map/ppermute | solution.py:26
  59.3 1.7 %collective-permute-done.19 = f32[192,128]{1,0:T(8,128)S(1)} collective-permute-done((f32[192,128]{1,0:T(8,128)S(1)}, f32[192,128]{1,0:T(8,128)S(1)}, u32[]{:S(2)}, u32[]{:S(2)}) %collective-permute-start.19) | collective-permute-done | bytes 98336 | tf_op jit(solution)/shard_map/ppermute | solution.py:355
  61.0 2.0 %collective-permute-done.18 = f32[192,128]{1,0:T(8,128)S(1)} collective-permute-done((f32[192,128]{1,0:T(8,128)S(1)}, f32[192,128]{1,0:T(8,128)S(1)}, u32[]{:S(2)}, u32[]{:S(2)}) %collective-permute-start.18) | collective-permute-done | bytes 98336 | tf_op jit(solution)/shard_map/ppermute | solution.py:355
  63.1 0.4 fusion.2
  63.7 0.7 copy.28
  64.5 3.6 %all-to-all-start.1 = ((f32[8,3,16,128]{3,2,1,0:T(8,128)}), f32[8,3,16,128]{3,2,1,0:T(8,128)S(1)}, u32[]{:S(2)}, u32[]{:S(2)}) async-start(f32[8,3,16,128]{3,2,1,0:T(8,128)} %bitcast.48), calls=%async_computation.1 | async-start | bytes 393216 | tf_op jit(solution)/shard_map/all_to_all | solution.py:400
  68.1 8.1 %all-to-all-done.1 = f32[8,3,16,128]{3,2,1,0:T(8,128)S(1)} async-done(((f32[8,3,16,128]{3,2,1,0:T(8,128)}), f32[8,3,16,128]{3,2,1,0:T(8,128)S(1)}, u32[]{:S(2)}, u32[]{:S(2)}) %all-to-all-start.1) | async-done | bytes 196640 | tf_op jit(solution)/shard_map/all_to_all | solution.py:400
  76.3 1.1 %copy.19 = f32[128,8,128]{2,1,0:T(8,128)} copy(f32[128,8,128]{2,0,1:T(8,128)S(1)} %maximum_bitcast_fusion) | data formatting | bytes 1048576
  (49 shorter events, 1.7 us)
Async XLA Ops:
  2.9 8.1 %copy-start.5 = (s32[64,1]{0,1:T(1,128)S(1)}, s32[64,1]{0,1:T(1,128)}, u32[]{:S(2)}) copy-start(s32[64,1]{0,1:T(1,128)} %param.15) | copy-start | bytes 772
  2.9 8.1 %collective-permute-start = (f32[328,128]{1,0:T(8,128)}, f32[328,128]{1,0:T(8,128)S(1)}, u32[]{:S(2)}, u32[]{:S(2)}) collective-permute-start(f32[328,128]{1,0:T(8,128)} %home_array.1.refs_0_.refs_1_.refs_7_), channel_id=1, source_target_pairs={{0,1},{1,0},{2,3},{3,2},{4,5},{5,4},{6,7},{7,6},{8,9},{9,8},{10,11... | collective-permute-start | bytes 503816 | tf_op jit(solution)/shard_map/ppermute | solution.py:26
  5.9 5.3 %collective-permute-start.1 = (f32[328,128]{1,0:T(8,128)}, f32[328,128]{1,0:T(8,128)S(1)}, u32[]{:S(2)}, u32[]{:S(2)}) collective-permute-start(f32[328,128]{1,0:T(8,128)} %home_array.1.refs_0_.refs_1_.refs_7_), channel_id=1, source_target_pairs={{0,2},{2,0},{1,3},{3,1},{4,6},{6,4},{5,7},{7,5},{8,10},{10,8},{9,1... | collective-permute-start | bytes 503816 | tf_op jit(solution)/shard_map/ppermute | solution.py:26
  5.9 9.6 %collective-permute-start.3 = (f32[328,128]{1,0:T(8,128)}, f32[328,128]{1,0:T(8,128)S(1)}, u32[]{:S(2)}, u32[]{:S(2)}) collective-permute-start(f32[328,128]{1,0:T(8,128)} %home_array.1.refs_0_.refs_1_.refs_7_), channel_id=1, source_target_pairs={{0,4},{4,0},{8,12},{12,8},{16,20},{20,16},{24,28},{28,24},{1,5},{5... | collective-permute-start | bytes 503816 | tf_op jit(solution)/shard_map/ppermute | solution.py:355
  7.4 9.3 %collective-permute-start.4 = (f32[328,128]{1,0:T(8,128)}, f32[328,128]{1,0:T(8,128)S(1)}, u32[]{:S(2)}, u32[]{:S(2)}) collective-permute-start(f32[328,128]{1,0:T(8,128)} %home_array.1.refs_0_.refs_1_.refs_7_), channel_id=1, source_target_pairs={{4,8},{8,4},{12,16},{16,12},{20,24},{24,20},{28,0},{0,28},{5,9},{9... | collective-permute-start | bytes 503816 | tf_op jit(solution)/shard_map/ppermute | solution.py:355
  11.0 1.4 %collective-permute-start.2 = (f32[328,128]{1,0:T(8,128)S(1)}, f32[328,128]{1,0:T(8,128)S(1)}, u32[]{:S(2)}, u32[]{:S(2)}) collective-permute-start(f32[328,128]{1,0:T(8,128)S(1)} %collective-permute-done.refs_1_.refs_2_.refs_8_), channel_id=1, source_target_pairs={{0,2},{2,0},{1,3},{3,1},{4,6},{6,4},{5,7},{7,5},{8,10},{10,8},{9,1... | collective-permute-start | bytes 503816 | tf_op jit(solution)/shard_map/ppermute | solution.py:26
  12.4 0.9 %copy-start = (f32[328,128]{1,0:T(8,128)S(1)}, f32[328,128]{1,0:T(8,128)}, u32[]{:S(2)}) copy-start(f32[328,128]{1,0:T(8,128)} %home_array.1.refs_0_.refs_1_.refs_7_) | copy-start | bytes 503812
  13.3 3.4 %copy-start.1 = (f32[328,128]{1,0:T(8,128)S(1)}, f32[328,128]{1,0:T(8,128)}, u32[]{:S(2)}) copy-start(f32[328,128]{1,0:T(8,128)} %home_array.1.refs_0_.refs_1_.refs_7_) | copy-start | bytes 503812
  23.6 5.9 %collective-permute-start.6 = (f32[192,128]{1,0:T(8,128)S(1)}, f32[192,128]{1,0:T(8,128)S(1)}, u32[]{:S(2)}, u32[]{:S(2)}) collective-permute-start(f32[192,128]{1,0:T(8,128)S(1)} %get-tuple-element.17), channel_id=1, source_target_pairs={{0,2},{2,0},{1,3},{3,1},{4,6},{6,4},{5,7},{7,5},{8,10},{10,8},{9,1... | collective-permute-start | bytes 294920 | tf_op jit(solution)/shard_map/ppermute | solution.py:26
  23.9 8.9 %collective-permute-start.9 = (f32[192,128]{1,0:T(8,128)S(1)}, f32[192,128]{1,0:T(8,128)S(1)}, u32[]{:S(2)}, u32[]{:S(2)}) collective-permute-start(f32[192,128]{1,0:T(8,128)S(1)} %get-tuple-element.19), channel_id=1, source_target_pairs={{4,8},{8,4},{12,16},{16,12},{20,24},{24,20},{28,0},{0,28},{5,9},{9... | collective-permute-start | bytes 294920 | tf_op jit(solution)/shard_map/ppermute | solution.py:355
  29.2 5.6 %collective-permute-start.8 = (f32[192,128]{1,0:T(8,128)S(1)}, f32[192,128]{1,0:T(8,128)S(1)}, u32[]{:S(2)}, u32[]{:S(2)}) collective-permute-start(f32[192,128]{1,0:T(8,128)S(1)} %get-tuple-element.18), channel_id=1, source_target_pairs={{0,4},{4,0},{8,12},{12,8},{16,20},{20,16},{24,28},{28,24},{1,5},{5... | collective-permute-start | bytes 294920 | tf_op jit(solution)/shard_map/ppermute | solution.py:355
  29.2 5.6 %collective-permute-start.5 = (f32[192,128]{1,0:T(8,128)S(1)}, f32[192,128]{1,0:T(8,128)S(1)}, u32[]{:S(2)}, u32[]{:S(2)}) collective-permute-start(f32[192,128]{1,0:T(8,128)S(1)} %get-tuple-element.15), channel_id=1, source_target_pairs={{0,2},{2,0},{1,3},{3,1},{4,6},{6,4},{5,7},{7,5},{8,10},{10,8},{9,1... | collective-permute-start | bytes 294920 | tf_op jit(solution)/shard_map/ppermute | solution.py:26
  29.5 5.3 %copy-start.4 = (f32[64,3,128]{2,0,1:T(8,128)S(1)}, f32[64,3,128]{2,0,1:T(8,128)}, u32[]{:S(2)}) copy-start(f32[64,3,128]{2,0,1:T(8,128)} %param.9) | copy-start | bytes 294916
  29.5 5.3 %copy-start.2 = (f32[64,3,128]{2,0,1:T(8,128)S(1)}, f32[64,3,128]{2,0,1:T(8,128)}, u32[]{:S(2)}) copy-start(f32[64,3,128]{2,0,1:T(8,128)} %param.8) | copy-start | bytes 294916
  29.5 5.3 %collective-permute-start.7 = (f32[192,128]{1,0:T(8,128)S(1)}, f32[192,128]{1,0:T(8,128)S(1)}, u32[]{:S(2)}, u32[]{:S(2)}) collective-permute-start(f32[192,128]{1,0:T(8,128)S(1)} %add.62), channel_id=1, source_target_pairs={{0,1},{1,0},{2,3},{3,2},{4,5},{5,4},{6,7},{7,6},{8,9},{9,8},{10,11... | collective-permute-start | bytes 294920 | tf_op jit(solution)/shard_map/ppermute | solution.py:26
  34.9 4.8 %collective-permute-start.10 = (f32[192,128]{1,0:T(8,128)S(1)}, f32[192,128]{1,0:T(8,128)S(1)}, u32[]{:S(2)}, u32[]{:S(2)}) collective-permute-start(f32[192,128]{1,0:T(8,128)S(1)} %get-tuple-element.28.refs_1_), channel_id=1, source_target_pairs={{0,1},{1,0},{2,3},{3,2},{4,5},{5,4},{6,7},{7,6},{8,9},{9,8},{10,11... | collective-permute-start | bytes 294920 | tf_op jit(solution)/shard_map/ppermute | solution.py:26
  35.5 9.2 %collective-permute-start.11 = (f32[192,128]{1,0:T(8,128)S(1)}, f32[192,128]{1,0:T(8,128)S(1)}, u32[]{:S(2)}, u32[]{:S(2)}) collective-permute-start(f32[192,128]{1,0:T(8,128)S(1)} %get-tuple-element.28.refs_1_), channel_id=1, source_target_pairs={{0,2},{2,0},{1,3},{3,1},{4,6},{6,4},{5,7},{7,5},{8,10},{10,8},{9,1... | collective-permute-start | bytes 294920 | tf_op jit(solution)/shard_map/ppermute | solution.py:26
  35.5 9.2 %collective-permute-start.13 = (f32[192,128]{1,0:T(8,128)S(1)}, f32[192,128]{1,0:T(8,128)S(1)}, u32[]{:S(2)}, u32[]{:S(2)}) collective-permute-start(f32[192,128]{1,0:T(8,128)S(1)} %get-tuple-element.28.refs_1_), channel_id=1, source_target_pairs={{0,4},{4,0},{8,12},{12,8},{16,20},{20,16},{24,28},{28,24},{1,5},{5... | collective-permute-start | bytes 294920 | tf_op jit(solution)/shard_map/ppermute | solution.py:355
  37.2 7.6 %collective-permute-start.14 = (f32[192,128]{1,0:T(8,128)S(1)}, f32[192,128]{1,0:T(8,128)S(1)}, u32[]{:S(2)}, u32[]{:S(2)}) collective-permute-start(f32[192,128]{1,0:T(8,128)S(1)} %get-tuple-element.28.refs_1_), channel_id=1, source_target_pairs={{4,8},{8,4},{12,16},{16,12},{20,24},{24,20},{28,0},{0,28},{5,9},{9... | collective-permute-start | bytes 294920 | tf_op jit(solution)/shard_map/ppermute | solution.py:355
  39.6 5.2 %collective-permute-start.12 = (f32[192,128]{1,0:T(8,128)S(1)}, f32[192,128]{1,0:T(8,128)S(1)}, u32[]{:S(2)}, u32[]{:S(2)}) collective-permute-start(f32[192,128]{1,0:T(8,128)S(1)} %collective-permute-done.10.refs_2_), channel_id=1, source_target_pairs={{0,2},{2,0},{1,3},{3,1},{4,6},{6,4},{5,7},{7,5},{8,10},{10,8},{9,1... | collective-permute-start | bytes 294920 | tf_op jit(solution)/shard_map/ppermute | solution.py:26
  41.0 23.5 %all-to-all-start = ((f32[8,8,16,128]{3,2,1,0:T(8,128)}), f32[8,8,16,128]{3,2,1,0:T(8,128)S(1)}, u32[]{:S(2)}, u32[]{:S(2)}) async-start(f32[8,8,16,128]{3,2,1,0:T(8,128)} %bitcast.47), calls=%async_computation | async-start | bytes 1048576 | tf_op jit(solution)/shard_map/all_to_all | solution.py:400
  51.7 6.0 %collective-permute-start.16 = (f32[192,128]{1,0:T(8,128)S(1)}, f32[192,128]{1,0:T(8,128)S(1)}, u32[]{:S(2)}, u32[]{:S(2)}) collective-permute-start(f32[192,128]{1,0:T(8,128)S(1)} %get-tuple-element.23), channel_id=1, source_target_pairs={{0,2},{2,0},{1,3},{3,1},{4,6},{6,4},{5,7},{7,5},{8,10},{10,8},{9,1... | collective-permute-start | bytes 294920 | tf_op jit(solution)/shard_map/ppermute | solution.py:26
  52.0 9.0 %collective-permute-start.19 = (f32[192,128]{1,0:T(8,128)S(1)}, f32[192,128]{1,0:T(8,128)S(1)}, u32[]{:S(2)}, u32[]{:S(2)}) collective-permute-start(f32[192,128]{1,0:T(8,128)S(1)} %get-tuple-element.25), channel_id=1, source_target_pairs={{4,8},{8,4},{12,16},{16,12},{20,24},{24,20},{28,0},{0,28},{5,9},{9... | collective-permute-start | bytes 294920 | tf_op jit(solution)/shard_map/ppermute | solution.py:355
  57.5 5.5 %collective-permute-start.18 = (f32[192,128]{1,0:T(8,128)S(1)}, f32[192,128]{1,0:T(8,128)S(1)}, u32[]{:S(2)}, u32[]{:S(2)}) collective-permute-start(f32[192,128]{1,0:T(8,128)S(1)} %get-tuple-element.24), channel_id=1, source_target_pairs={{0,4},{4,0},{8,12},{12,8},{16,20},{20,16},{24,28},{28,24},{1,5},{5... | collective-permute-start | bytes 294920 | tf_op jit(solution)/shard_map/ppermute | solution.py:355
  57.5 5.5 %collective-permute-start.15 = (f32[192,128]{1,0:T(8,128)S(1)}, f32[192,128]{1,0:T(8,128)S(1)}, u32[]{:S(2)}, u32[]{:S(2)}) collective-permute-start(f32[192,128]{1,0:T(8,128)S(1)} %get-tuple-element.21), channel_id=1, source_target_pairs={{0,2},{2,0},{1,3},{3,1},{4,6},{6,4},{5,7},{7,5},{8,10},{10,8},{9,1... | collective-permute-start | bytes 294920 | tf_op jit(solution)/shard_map/ppermute | solution.py:26
  57.7 5.4 %collective-permute-start.17 = (f32[192,128]{1,0:T(8,128)S(1)}, f32[192,128]{1,0:T(8,128)S(1)}, u32[]{:S(2)}, u32[]{:S(2)}) collective-permute-start(f32[192,128]{1,0:T(8,128)S(1)} %add.69), channel_id=1, source_target_pairs={{0,1},{1,0},{2,3},{3,2},{4,5},{5,4},{6,7},{7,6},{8,9},{9,8},{10,11... | collective-permute-start | bytes 294920 | tf_op jit(solution)/shard_map/ppermute | solution.py:26
  63.1 0.6 copy-start.3
  64.5 11.7 %all-to-all-start.1 = ((f32[8,3,16,128]{3,2,1,0:T(8,128)}), f32[8,3,16,128]{3,2,1,0:T(8,128)S(1)}, u32[]{:S(2)}, u32[]{:S(2)}) async-start(f32[8,3,16,128]{3,2,1,0:T(8,128)} %bitcast.48), calls=%async_computation.1 | async-start | bytes 393216 | tf_op jit(solution)/shard_map/all_to_all | solution.py:400
